TPU v7x, 512 devices: a whole 4x8x8 slice. The times are simulated.
512 devices in a mesh: dp: 4 (over z_hi, core), ctx: 32 (over z_lo, y), tp: 4 (over x).
Axes of the slice: x: 4, y: 8, z: 8 (z_hi: 2, z_lo: 4; z = z_hi * 4 + z_lo), core: 2. Of those that a mesh axis runs over, the one named last changes fastest.
Arguments:
- q_feat: bfloat16 [32768, 4096], P(('dp', 'ctx'), 'tp'), parts along dimension 0, may hold values from -6 to 6
- k_feat: bfloat16 [32768, 4096], P(('dp', 'ctx'), 'tp'), parts along dimension 0, may hold values from -6 to 6
- v_feat: bfloat16 [32768, 4096], P(('dp', 'ctx'), 'tp'), parts along dimension 0, may hold values from -6 to 6
- short_taps: float32 [3, 3, 4096], P(None, None, 'tp'), may hold values from -3 to 3
- decay_rate: float32 [4096, 16], P('tp'), may hold values from 2.4414063e-05 to 0.04
- residue: float32 [4096, 16], P('tp'), may hold values from -4 to 4
- out_weight: bfloat16 [4096, 4096], P('tp', 'ctx'), may hold values from -0.8125 to 0.8125
- direction: float32 [4096], replicated, may hold values from -120 to 120
Outputs:
- ablated: bfloat16 [32768, 4096], P(('dp', 'ctx'), 'tp'), parts along dimension 0
- feature_level: float32 [32768], P(('dp', 'ctx')), parts along dimension 0
There are 4 independent parts, one for each index of `dp`. A program takes and returns all parts, laid end to end along the dimension named above; an argument that names none is the same for every part. Nothing has to cross between parts.
All inputs are finite; a program needn't handle non-finite values.
Results may differ from a plain program's by a relative error of at most 0.019.
Values may be sent and summed in bfloat16 or wider, within the bound.
A program may use at most 128 MiB of HBM per device.

v0:
```python
import math

import jax
import jax.numpy as jnp
from jax import lax
from jax.sharding import PartitionSpec as P

EPSILON = 1e-06
HIGHEST = lax.Precision.HIGHEST


def short_filter(values, prefix, filter_taps):
    length = values.shape[1]
    width = filter_taps.shape[0]
    padded = jnp.concatenate([prefix, values], axis=1).astype(jnp.float32)
    summed = jnp.zeros((values.shape[0], length), jnp.float32)
    for offset in range(width):
        summed = (
            summed
            + filter_taps[offset][:, None]
            * padded[:, width - 1 - offset : width - 1 - offset + length]
        )
    return summed


def combine_modes(earlier, later):
    return (earlier[0] * later[0], earlier[1] * later[0] + later[1])


def modal_filter(signal, rate, gain, receive):
    width, length = signal.shape
    mode_count = rate.shape[1]
    block = math.gcd(length, 128)
    block_count = length // block
    steps_in = jnp.arange(block, dtype=jnp.float32)
    growing = jnp.exp(rate[:, :, None] * steps_in[None, None, :])
    shrinking = gain[:, :, None] * jnp.exp(-rate[:, :, None] * steps_in[None, None, :])
    start_table = gain[:, :, None] * jnp.exp(-rate[:, :, None] * (steps_in + 1.0)[None, None, :])
    source = lax.broadcasted_iota(jnp.int32, (block, block), 0)
    target = lax.broadcasted_iota(jnp.int32, (block, block), 1)
    lower_mask = (source <= target).astype(jnp.float32)
    blocks = signal.reshape(width, 1, block_count, block)
    scaled = (blocks * growing[:, :, None, :]).reshape(width * mode_count * block_count, block)
    running = jnp.dot(scaled, lower_mask, precision=HIGHEST).reshape(
        width, mode_count, block_count, block
    )
    inside = jnp.einsum("cmnt,cmt->cnt", running, shrinking, precision=HIGHEST)
    block_ends = running[:, :, :, block - 1] * jnp.exp(-rate * (block - 1.0))[:, :, None]
    block_ends = jnp.transpose(block_ends, (2, 0, 1))
    block_decay = jnp.broadcast_to(jnp.exp(-rate * block)[None], block_ends.shape)
    decays, states = lax.associative_scan(combine_modes, (block_decay, block_ends), axis=0)
    incoming = receive(decays[-1], states[-1])
    states = states + decays * incoming[None]
    starts = jnp.concatenate([incoming[None], states[:-1]], axis=0)
    carried = jnp.einsum("ncm,cmt->cnt", starts, start_table, precision=HIGHEST)
    return (inside + carried).reshape(width, length)


def shards(q_feat, k_feat, v_feat, short_taps, decay_rate, residue, out_weight, direction):
    tokens_here, channels_here = q_feat.shape
    mode_count = decay_rate.shape[1]
    edge_rows = short_taps.shape[1] - 1
    gain_all = residue * jnp.sqrt(-jnp.expm1(-2.0 * decay_rate)) * mode_count ** (-0.5)
    stacked = jnp.transpose(jnp.stack([q_feat, k_feat, v_feat]), (0, 2, 1))
    group_width = channels_here // lax.axis_size("ctx")
    first_channel = lax.axis_index("ctx") * group_width
    columns = lax.all_to_all(stacked, "ctx", split_axis=1, concat_axis=2, tiled=True)
    taps_here = lax.dynamic_slice_in_dim(short_taps, first_channel, group_width, 2)
    rate_here = lax.dynamic_slice_in_dim(decay_rate, first_channel, group_width, 0)
    gain_here = lax.dynamic_slice_in_dim(gain_all, first_channel, group_width, 0)
    zero_rows = jnp.zeros((group_width, edge_rows), jnp.bfloat16)
    query_short = short_filter(columns[0], zero_rows, taps_here[0])
    key_short = short_filter(columns[1], zero_rows, taps_here[1])
    value_short = short_filter(columns[2], zero_rows, taps_here[2])

    def no_state(decay_total, state_total):
        return jnp.zeros_like(state_total)

    mixed = modal_filter(key_short * value_short, rate_here, gain_here, no_state)
    gated_columns = (query_short * mixed).astype(jnp.bfloat16)
    gated = lax.all_to_all(gated_columns, "ctx", split_axis=1, concat_axis=0, tiled=True)
    partial_terms = lax.dot_general(
        gated,
        lax.all_gather(out_weight, "ctx", axis=1, tiled=True),
        (((0,), (0,)), ((), ())),
        preferred_element_type=jnp.float32,
    )
    summed = lax.psum_scatter(
        partial_terms.astype(jnp.bfloat16), "tp", scatter_dimension=1, tiled=True
    ).astype(jnp.float32)
    width_here = summed.shape[1]
    direction_here = lax.dynamic_slice_in_dim(
        direction, lax.axis_index("tp") * width_here, width_here, 0
    )
    norm_total = jnp.sum(direction * direction) + EPSILON
    local_inner = jnp.dot(summed, direction_here, precision=HIGHEST)
    feature_level = lax.psum(local_inner, "tp") / norm_total
    ablated = (summed - feature_level[:, None] * direction_here[None, :]).astype(jnp.bfloat16)
    return (ablated, feature_level)


def solution(mesh):
    placed = (
        P(("dp", "ctx"), "tp"),
        P(("dp", "ctx"), "tp"),
        P(("dp", "ctx"), "tp"),
        P(None, None, "tp"),
        P("tp", None),
        P("tp", None),
        P("tp", "ctx"),
        P(),
    )
    return jax.shard_map(
        shards,
        mesh=mesh,
        in_specs=placed,
        out_specs=(P(("dp", "ctx"), "tp"), P(("dp", "ctx"))),
        check_vma=False,
    )
```

profile of v0, /device:TPU:1, one launch (start us, length us, event | category | flops | bytes accessed | tf_op | source)
XLA Modules:
  0.0 340.3 jit_solution(7930708298426711348)
XLA Ops:
  7.9 1.5 maximum_bitcast_fusion
  9.4 2.6 copy.235
  12.1 13.5 %all-to-all-start = ((bf16[3,1024,256]{2,0,1:T(4,128)(2,1)}), bf16[3,1024,256]{2,0,1:T(4,128)(2,1)S(1)}, u32[]{:S(2)}, u32[]{:S(2)}) async-start(bf16[3,1024,256]{2,0,1:T(4,128)(2,1)} %copy.235), calls=%async_computation | async-start | bytes 4194304 | tf_op jit(solution)/shard_map/all_to_all | solution.py:67
  25.6 0.8 multiply_multiply_fusion
  28.1 0.9 copy.250
  29.1 0.9 copy.259
  30.0 0.9 copy.260
  30.9 0.9 copy.261
  31.8 0.9 copy.262
  32.8 11.4 %pad.94 = f32[4,32,16]{0,2,1:T(8,128)} pad(f32[2,32,16]{0,2,1:T(8,128)S(1)} %pad_add_fusion.1, f32[]{:T(128)} %constant.11.clone.1), padding=1_0_1x0_0_0x0_0_0 | pad | bytes 12292 | tf_op jit(solution)/shard_map/pad | solution.py:51
  44.3 0.9 fusion.29
  45.2 1.1 multiply_exponential_fusion
  46.2 40.5 %all-to-all-done = bf16[3,1024,256]{2,0,1:T(4,128)(2,1)S(1)} async-done(((bf16[3,1024,256]{2,0,1:T(4,128)(2,1)}), bf16[3,1024,256]{2,0,1:T(4,128)(2,1)S(1)}, u32[]{:S(2)}, u32[]{:S(2)}) %all-to-all-start) | async-done | bytes 1572896 | tf_op jit(solution)/shard_map/all_to_all | solution.py:67
  87.0 0.9 fusion.38
  88.4 1.2 fusion.7
  90.7 9.0 %multiply_reduce_fusion = (f32[32,128,64]{1,2,0:T(8,128)S(1)}, f32[32,16,64,128]{3,2,1,0:T(8,128)S(1)}) fusion(f32[32,128,16]{1,2,0:T(8,128)S(1)} %copy-done.6, f32[32,16,128]{2,1,0:T(8,128)S(1)} %copy-done.5, f32[32,64,128]{2,1,0:T(8,128)S(1)} %bitcast.97), kind=kOutput, calls=%fused_computation.1 | convolution fusion | flops 6454788096 | bytes 19398656 | tf_op jit(solution)/shard_map/dot_general | solution.py:44
  99.7 9.0 %slice_reduce_fusion = f32[32,16,64]{2,1,0:T(8,128)S(1)} fusion(f32[32,16,64,128]{3,2,1,0:T(8,128)S(1)} %get-tuple-element.44), kind=kLoop, calls=%fused_computation | loop fusion | bytes 262144 | tf_op jit(solution)/shard_map/slice | solution.py:48
  108.9 3.2 slice.263
  112.1 3.3 slice.265
  115.6 1.8 slice.267
  117.4 1.9 slice.269
  119.4 1.1 slice.271
  120.5 1.2 slice.273
  122.6 0.8 slice.277
  124.1 0.8 slice.281
  125.0 1.7 slice.288
  126.6 1.9 slice.291
  128.5 2.3 slice.294
  130.8 3.7 %slice.297 = f32[31,32,16]{0,2,1:T(8,128)} slice(f32[64,32,16]{0,2,1:T(8,128)S(1)} %multiply_bitcast_fusion), slice={[2:64:2], [0:32:1], [0:16:1]} | slice | bytes 126976 | tf_op jit(solution)/shard_map/slice | solution.py:51
  134.8 0.8 pad_add_fusion
  135.7 12.4 %pad.82 = f32[4,32,16]{0,2,1:T(8,128)S(1)} pad(f32[2,32,16]{0,2,1:T(8,128)} %pad_add_fusion, f32[]{:T(128)} %constant.11.clone.1), padding=1_0_1x0_0_0x0_0_0 | pad | bytes 12292 | tf_op jit(solution)/shard_map/pad | solution.py:51
  148.0 2.2 fusion.39
  150.3 2.3 pad.93
  152.6 1.2 pad_maximum_fusion
  153.8 2.3 pad.81
  157.6 1.1 fusion.16
  158.8 2.4 pad.95
  161.2 12.4 %pad.96 = f32[8,32,16]{0,2,1:T(8,128)S(1)} pad(f32[4,32,16]{0,2,1:T(8,128)} %add.199, f32[]{:T(128)} %constant.11.clone.1), padding=1_0_1x0_0_0x0_0_0 | pad | bytes 24580 | tf_op jit(solution)/shard_map/pad | solution.py:51
  173.7 2.7 pad.98
  176.5 2.4 pad.83
  178.9 12.4 %pad.84 = f32[8,32,16]{0,2,1:T(8,128)S(1)} pad(f32[4,32,16]{0,2,1:T(8,128)} %add.189, f32[]{:T(128)} %constant.11.clone.1), padding=1_0_1x0_0_0x0_0_0 | pad | bytes 24580 | tf_op jit(solution)/shard_map/pad | solution.py:51
  192.1 1.1 fusion.15
  193.2 1.1 pad_maximum_fusion.7
  194.3 2.7 pad.97
  197.0 3.2 pad.100
  200.3 2.7 pad.86
  203.2 2.7 pad.85
  206.6 1.1 fusion.14
  207.8 3.2 pad.99
  211.1 12.5 %pad.162 = f32[64,32,16]{0,2,1:T(8,128)} pad(f32[32,32,16]{0,2,1:T(8,128)S(1)} %add.202, f32[]{:T(128)} %constant.11.clone.1), padding=1_0_1x0_0_0x0_0_0 | pad | bytes 196612
  223.7 3.2 pad.87
  226.9 3.2 pad.88
  230.2 12.5 %pad.163 = f32[64,32,16]{0,2,1:T(8,128)} pad(f32[32,32,16]{0,2,1:T(8,128)S(1)} %add.195, f32[]{:T(128)} %constant.11.clone.1), padding=1_0_1x0_0_0x0_0_0 | pad | bytes 196612
  242.7 1.1 fusion.13
  244.1 4.3 %pad.129 = f32[63,32,16]{0,2,1:T(8,128)S(1)} pad(f32[32,32,16]{0,2,1:T(8,128)S(1)} %pad_maximum_fusion.4, f32[]{:T(128)} %constant.11.clone.1), padding=0_0_1x0_0_0x0_0_0 | pad | bytes 194564 | tf_op jit(solution)/shard_map/slice | solution.py:54
  248.3 1.1 pad_maximum_fusion.9
  249.4 4.3 %pad.127 = f32[63,32,16]{0,2,1:T(8,128)S(1)} pad(f32[32,32,16]{0,2,1:T(8,128)S(1)} %pad_maximum_fusion.9, f32[]{:T(128)} %constant.11.clone.1), padding=0_0_1x0_0_0x0_0_0 | pad | bytes 194564 | tf_op jit(solution)/shard_map/slice | solution.py:54
  253.8 2.1 convolution_add_fusion
  256.9 22.1 %all_to_all.34 = bf16[32,32,256]{2,0,1:T(8,128)(2,1)S(1)} all-to-all(bf16[32,32,256]{2,0,1:T(8,128)(2,1)S(1)} %bitcast.103), channel_id=1, replica_groups=mesh['dp'=4,'ctx'=32,'tp'=4] {'ctx'}, dimensions={1} | all-to-all | bytes 1048576 | tf_op jit(solution)/shard_map/all_to_all | solution.py:81
  279.0 7.2 %convolution_convert_fusion = bf16[256,4096]{1,0:T(8,128)(2,1)} fusion(bf16[1024,256]{1,0:T(8,128)(2,1)S(1)} %bitcast.99, bf16[1024,4096]{1,0:T(8,128)(2,1)} %all-gather.2.cloned.1.call-done), kind=kOutput, calls=%fused_computation.6 | convolution fusion | flops 2148532224 | bytes 11010048 | tf_op jit(solution)/shard_map/dot_general | solution.py:82
  288.1 35.3 %reduce-scatter.2.cloned.1.call-done = bf16[256,1024]{1,0:T(8,128)(2,1)} async-done(((bf16[256,4096]{1,0:T(8,128)(2,1)}), bf16[256,1024]{1,0:T(8,128)(2,1)}) %reduce-scatter.2.cloned.1.call-update) | async-done | bytes 524304 | tf_op jit(solution)/shard_map/reduce_scatter | solution.py:88
  323.3 1.5 fusion.40
  324.9 6.6 %psum.7 = f32[256]{0:T(256)S(1)} all-reduce(f32[256]{0:T(256)S(1)} %bitcast.112), channel_id=1, replica_groups=mesh['dp'=4,'ctx'=32,'tp'=4] {'tp'}, use_global_device_ids=true, to_apply=%region_1.0 | all-reduce | flops 256 | bytes 2048 | tf_op jit(solution)/shard_map/psum | solution.py:97
  331.5 2.0 subtract_convert_fusion
  (86 shorter events, 13.2 us)
Async XLA Ops:
  7.2 271.8 %all-gather.2.cloned.1.call-start = ((), (), s32[]{:S(2)}) async-start(), calls=%async_computation.3 | async-start | bytes 8650752 | tf_op jit(solution)/shard_map/all_gather | solution.py:84
  12.1 74.7 %all-to-all-start = ((bf16[3,1024,256]{2,0,1:T(4,128)(2,1)}), bf16[3,1024,256]{2,0,1:T(4,128)(2,1)S(1)}, u32[]{:S(2)}, u32[]{:S(2)}) async-start(bf16[3,1024,256]{2,0,1:T(4,128)(2,1)} %copy.235), calls=%async_computation | async-start | bytes 4194304 | tf_op jit(solution)/shard_map/all_to_all | solution.py:67
  25.5 297.8 %reduce-scatter.2.cloned.1.call-start = ((), (), s32[]{:S(2)}) async-start(), calls=%async_computation.4 | async-start | bytes 2621440 | tf_op jit(solution)/shard_map/reduce_scatter | solution.py:88
  29.1 59.3 %copy-start.3 = (f32[1,32,16]{0,2,1:T(8,128)}, f32[1,32,16]{0,2,1:T(8,128)S(1)}, u32[]{:S(2)}) copy-start(f32[1,32,16]{0,2,1:T(8,128)S(1)} %copy.256) | copy-start | bytes 6148
  89.7 1.0 copy-start.5
  89.7 1.0 copy-start.6
  134.8 0.8 copy-start.1
  148.0 2.2 copy-start.2
  148.0 8.1 %copy-start = (f32[4,32,16]{0,2,1:T(8,128)S(1)}, f32[4,32,16]{0,2,1:T(8,128)}, u32[]{:S(2)}) copy-start(f32[4,32,16]{0,2,1:T(8,128)} %pad.94) | copy-start | bytes 24580
  156.1 2.6 copy-start.12
  193.2 7.1 %copy-start.10 = (f32[8,32,16]{0,2,1:T(8,128)S(1)}, f32[8,32,16]{0,2,1:T(8,128)}, u32[]{:S(2)}) copy-start(f32[8,32,16]{0,2,1:T(8,128)} %add.191) | copy-start | bytes 49156
  205.8 1.9 copy-start.11
  207.7 19.2 %copy-start.9 = (f32[16,32,16]{0,2,1:T(8,128)S(1)}, f32[16,32,16]{0,2,1:T(8,128)}, u32[]{:S(2)}) copy-start(f32[16,32,16]{0,2,1:T(8,128)} %add.193) | copy-start | bytes 98308
  242.7 10.9 %copy-start.4 = (bf16[1,32,32,256]{3,1,2,0:T(8,128)(2,1)S(1)}, bf16[1,32,32,256]{3,1,2,0:T(8,128)(2,1)}, u32[]{:S(2)}) copy-start(bf16[1,32,32,256]{3,1,2,0:T(8,128)(2,1)} %get-tuple-element.4) | copy-start | bytes 1572868
  243.9 9.8 %copy-start.7 = (f32[64,32,16]{0,2,1:T(8,128)S(1)}, f32[64,32,16]{0,2,1:T(8,128)}, u32[]{:S(2)}) copy-start(f32[64,32,16]{0,2,1:T(8,128)} %pad.162) | copy-start | bytes 393220
  243.9 9.8 %copy-start.8 = (f32[64,32,16]{0,2,1:T(8,128)S(1)}, f32[64,32,16]{0,2,1:T(8,128)}, u32[]{:S(2)}) copy-start(f32[64,32,16]{0,2,1:T(8,128)} %pad.163) | copy-start | bytes 393220
  286.1 0.7 copy-start.13
  331.5 2.0 copy-start.14
Sparse Core Ops, SparseCore 0:
  10.0 195.8 all-gather.1
  286.3 37.0 reduce-scatter.1
where the time goes:
time: 344 us; the launch traced here: 340 us
  local copies, waits for them, and re-layouts  161 us (47%)
  waiting for transfers between devices  76.5 us (22%)
  blocking collectives  28.6 us (8%)
  other arithmetic  25.4 us (7%)
  matrix products  19.7 us (6%)
  between operations  15.3 us (4%)
  starting transfers between devices  13.5 us (4%)
    pad x16, local copies, waits for them, and re-layouts, modal_filter(): lax.associative_scan(combine_modes, (block_decay, block_ends), axis=0)  81.5 us
    all_to_all x1, waiting for transfers between devices, shards(): lax.all_to_all(stacked, 'ctx', split_axis=1, concat_axis=2, tiled=True)  40.5 us
    reduce_scatter x1, waiting for transfers between devices, shards(): lax.psum_scatter(partial_terms.astype(jnp.bfloat16), 'tp', scatter_dimens...  35.3 us
    slice x17, local copies, waits for them, and re-layouts, modal_filter(): lax.associative_scan(combine_modes, (block_decay, block_ends), axis=0)  27.7 us
    unnamed x36, local copies, waits for them, and re-layouts  26.9 us
    all_to_all x1, blocking collectives, shards(): lax.all_to_all(gated_columns, 'ctx', split_axis=1, concat_axis=0, tiled=T...  22.1 us
    all_to_all x1, starting transfers between devices, shards(): lax.all_to_all(stacked, 'ctx', split_axis=1, concat_axis=2, tiled=True)  13.5 us
    slice x1, local copies, waits for them, and re-layouts, modal_filter(): running[:, :, :, block - 1] * jnp.exp(-rate * (block - 1.0))[:, :, None]  9.04 us
  transfers between devices with their start and end apart: 3, of which 2 were waited for; matrix products, arithmetic and copies ran while one was open for 57% of the time, Pallas kernels for 0%

commit v1 on v0

v1 whole, which is shorter than its diff:
```python
import jax
import jax.numpy as jnp
from jax import lax
from jax.experimental import pallas as pl
from jax.experimental.pallas import tpu as pltpu
from jax.sharding import PartitionSpec as P

EPSILON = 1e-06
HIGHEST = lax.Precision.HIGHEST
MODES = 16
GROUPS = 8
TOKENS = 256
WIDTH = 1024
PITCH = TOKENS + 8
NY = 8
NZ = 4
NX = 4


def kernel(
    q_ref, k_ref, v_ref, taps_ref, rate_ref, gain_ref, w_ref, dir_ref,
    out_ref, level_ref,
    xq, xk, xv, qs, ys, gf, gb, state, decay, carry,
    halo_out, halo_in, st_out, st_in, tot_out, tot_in,
    wg, part_o, part_r, part_l, part_own, mid_r, mid_l, from_l, from_r,
    inner_acc, inner_out, inner_in,
    halo_sem, y_send, y_recv, z_send, z_recv, w_send, w_recv,
    s_send, s_recv, x_send, x_recv, i_send, i_recv,
):
    dp = lax.axis_index("dp")
    ctx = lax.axis_index("ctx")
    x = lax.axis_index("tp")
    z_hi = dp // 2
    core = dp % 2
    z = ctx // NY
    y = ctx % NY
    z_all = z_hi * NZ + z

    def at_y(d):
        return (dp, z * NY + (y + d) % NY, x)

    def at_z(d):
        return (dp, ((z + d) % NZ) * NY + y, x)

    def on_z_ring(d):
        other = (z_all + d + 2 * NZ) % (2 * NZ)
        return ((other // NZ) * 2 + core, (other % NZ) * NY + y, x)

    def at_x(d):
        return (dp, ctx, (x + d) % NX)

    sibling = (z_hi * 2 + 1 - core, ctx, x)
    after = (dp, (ctx + 1) % (NY * NZ), x)
    before = (dp, (ctx + NY * NZ - 1) % (NY * NZ), x)

    def remote(src, dst, send, recv, target):
        return pltpu.make_async_remote_copy(
            src_ref=src, dst_ref=dst, send_sem=send, recv_sem=recv,
            device_id=target, device_id_type=pl.DeviceIdType.MESH,
        )

    barrier = pltpu.get_barrier_semaphore()
    partners = (
        [at_y(d) for d in range(1, NY)]
        + [at_z(d) for d in range(1, NZ)]
        + [on_z_ring(1), on_z_ring(-1)]
        + [at_x(d) for d in range(1, NX)]
        + [sibling, after, before]
    )
    for target in partners:
        pl.semaphore_signal(
            barrier, inc=1, device_id=target, device_id_type=pl.DeviceIdType.MESH
        )
    wg[z, y, core] = w_ref[pl.ds(pl.multiple_of(core * 512, 512), 512), :]
    halo_out[0:2, :] = q_ref[TOKENS - 16:, :].astype(jnp.float32)[14:16, :]
    halo_out[2:4, :] = k_ref[TOKENS - 16:, :].astype(jnp.float32)[14:16, :]
    halo_out[4:6, :] = v_ref[TOKENS - 16:, :].astype(jnp.float32)[14:16, :]
    halo_out[6:8, :] = jnp.zeros((2, WIDTH), jnp.float32)
    pl.semaphore_wait(barrier, len(partners))

    def zz(d):
        return (z + d + NZ) % NZ

    def yy(d):
        return (y + d + NY) % NY

    lo, hi = pl.ds(0, 256), pl.ds(256, 256)
    sent = [
        [
            (z, y, 0), (z, y, 0),
            (zz(-1), y, 0, lo), (zz(1), y, 0, hi),
            (slice(None), y, 0), (slice(None), y, 0),
            (slice(None), yy(-1), 0), (slice(None), yy(1), 0),
            (slice(None), yy(-2), 0), (slice(None), yy(2), 0),
            (pl.ds(0, 2), yy(-3), 0), (pl.ds(2, 2), yy(3), 0),
        ],
        [
            (z, y, 1), (z, y, 1),
            (z, yy(-1), 1), (z, yy(1), 1),
            (z, yy(-2), 1), (z, yy(2), 1),
            (z, yy(-3), 1, lo), (z, yy(3), 1, hi),
            (z, slice(None), 1), (z, slice(None), 1),
            (zz(-1), pl.ds(0, 4), 1), (zz(1), pl.ds(4, 4), 1),
        ],
    ]
    got = [
        [
            (zz(-1), y, 0), (zz(1), y, 0),
            (zz(2), y, 0, lo), (zz(2), y, 0, hi),
            (slice(None), yy(-1), 0), (slice(None), yy(1), 0),
            (slice(None), yy(-2), 0), (slice(None), yy(2), 0),
            (slice(None), yy(-3), 0), (slice(None), yy(3), 0),
            (pl.ds(0, 2), yy(4), 0), (pl.ds(2, 2), yy(4), 0),
        ],
        [
            (z, yy(-1), 1), (z, yy(1), 1),
            (z, yy(-2), 1), (z, yy(2), 1),
            (z, yy(-3), 1), (z, yy(3), 1),
            (z, yy(4), 1, lo), (z, yy(4), 1, hi),
            (zz(-1), slice(None), 1), (zz(1), slice(None), 1),
            (zz(2), pl.ds(0, 4), 1), (zz(2), pl.ds(4, 4), 1),
        ],
    ]
    axis_of = [["z"] * 4 + ["y"] * 8, ["y"] * 8 + ["z"] * 4]
    to_sibling = [
        [(2, [(slice(None), y, 0)])]
        + [(3, got[0][4:6]), (4, got[0][6:8]), (5, got[0][8:10]), (6, got[0][10:12])],
        [(4, [(z, slice(None), 1)]), (5, got[1][8:10]), (6, got[1][10:12])],
    ]

    def ring(role, index, slot):
        sign = 1 if index % 2 == 0 else -1
        target = at_y(NY + sign) if axis_of[role][index] == "y" else on_z_ring(sign)
        region = wg.at[slot]
        return remote(region, region, w_send.at[index], w_recv.at[index], target)

    def handed(role, wanted=None):
        flat = []
        for step, slots in to_sibling[role]:
            for slot in slots:
                flat.append((step, slot))
        return [
            remote(wg.at[slot], wg.at[slot], s_send.at[i], s_recv.at[i], sibling)
            for i, (step, slot) in enumerate(flat)
            if wanted is None or step == wanted
        ]

    def weight_step(step):
        for role in range(2):
            @pl.when(core == role)
            def _(role=role):
                if step > 0:
                    for index in (2 * step - 2, 2 * step - 1):
                        ring(role, index, got[role][index]).wait_recv()
                if step < 6:
                    for index in (2 * step, 2 * step + 1):
                        ring(role, index, sent[role][index]).start()
                for copy in handed(role, step):
                    copy.start()

    def weight_end():
        for role in range(2):
            @pl.when(core == role)
            def _(role=role):
                for copy in handed(1 - role):
                    copy.wait_recv()

    def weight_drain():
        for role in range(2):
            @pl.when(core == role)
            def _(role=role):
                for index in range(12):
                    ring(role, index, sent[role][index]).wait_send()
                for copy in handed(role):
                    copy.wait_send()

    halo = remote(halo_out, halo_in, halo_sem.at[0], halo_sem.at[1], after)
    halo.start()
    weight_step(0)

    for ref, full in ((q_ref, xq), (k_ref, xk), (v_ref, xv)):
        for g in range(GROUPS):
            full[g * PITCH + 8:(g + 1) * PITCH, :] = (
                ref[:, g * 128:(g + 1) * 128].astype(jnp.float32)
            )
    state[...] = jnp.zeros_like(state)
    decay[...] = jnp.exp(-rate_ref[...])
    halo.wait_recv()
    for i, full in enumerate((xq, xk, xv)):
        for g in range(GROUPS):
            rows = halo_in[2 * i:2 * i + 2, g * 128:(g + 1) * 128]
            full[g * PITCH + 6:g * PITCH + 8, :] = jnp.where(ctx > 0, rows, 0.0)
    weight_step(1)

    def row(t):
        return pl.ds(t, GROUPS, stride=PITCH)

    def tile(ref, i):
        return ref[i * GROUPS:(i + 1) * GROUPS, :]

    def filter_step(i, _):
        start = i * 8
        short = []
        for f, full in enumerate((xq, xk, xv)):
            values = [full[row(start + 6 + j), :] for j in range(10)]
            taps = [tile(taps_ref, f * 3 + o) for o in range(3)]
            short.append([
                taps[0] * values[j + 2] + taps[1] * values[j + 1] + taps[2] * values[j]
                for j in range(8)
            ])
        for j in range(8):
            qs[start + j] = short[0][j]
        signal = [short[1][j] * short[2][j] for j in range(8)]
        total = [None] * 8
        for m in range(MODES):
            h = tile(state, m)
            a = tile(decay, m)
            c = tile(gain_ref, m)
            for j in range(8):
                h = a * h + signal[j]
                term = c * h
                total[j] = term if total[j] is None else total[j] + term
            state[m * GROUPS:(m + 1) * GROUPS, :] = h
        for j in range(8):
            ys[start + j] = total[j]
        return 0

    half = TOKENS // 16
    lax.fori_loop(0, half, filter_step, 0)
    weight_step(2)
    lax.fori_loop(half, 2 * half, filter_step, 0)

    st_out[...] = state[...].astype(jnp.bfloat16)
    y_copies = [
        remote(st_out, st_in.at[y], y_send.at[d], y_recv.at[d], at_y(d))
        for d in range(1, NY)
    ]
    for copy in y_copies:
        copy.start()
    st_in[y] = st_out[...]
    weight_step(3)
    block_decay = jnp.exp(-float(TOKENS) * rate_ref[...])
    for d in range(1, NY):
        remote(
            st_out, st_in.at[yy(-d)], y_send.at[d], y_recv.at[d], at_y(d)
        ).wait_recv()
    prefix = jnp.zeros((128, 128), jnp.float32)
    total = jnp.zeros((128, 128), jnp.float32)
    for other in range(NY):
        arrived = st_in[other].astype(jnp.float32)
        total = total * block_decay + arrived
        prefix = jnp.where(other < y, prefix * block_decay + arrived, prefix)
    tot_out[...] = total.astype(jnp.bfloat16)
    z_copies = [
        remote(tot_out, tot_in.at[z], z_send.at[d], z_recv.at[d], at_z(d))
        for d in range(1, NZ)
    ]
    for copy in z_copies:
        copy.start()
    tot_in[z] = tot_out[...]
    carry[...] = prefix
    weight_step(4)
    group_decay = jnp.exp(-float(TOKENS * NY) * rate_ref[...])
    own_decay = jnp.exp(-(TOKENS * y).astype(jnp.float32) * rate_ref[...])
    for d in range(1, NZ):
        remote(
            tot_out, tot_in.at[zz(-d)], z_send.at[d], z_recv.at[d], at_z(d)
        ).wait_recv()
    earlier = jnp.zeros((128, 128), jnp.float32)
    for other in range(NZ):
        arrived = tot_in[other].astype(jnp.float32)
        earlier = jnp.where(other < z, earlier * group_decay + arrived, earlier)
    carry[...] = gain_ref[...] * (carry[...] + own_decay * earlier)

    def carry_step(i, _):
        start = i * 8
        total = [ys[start + j] for j in range(8)]
        for m in range(MODES):
            h = tile(carry, m)
            a = tile(decay, m)
            for j in range(8):
                h = a * h
                total[j] = total[j] + h
            carry[m * GROUPS:(m + 1) * GROUPS, :] = h
        for j in range(8):
            gf[row(start + j), :] = qs[start + j] * total[j]
        return 0

    lax.fori_loop(0, 2 * half, carry_step, 0)
    weight_step(5)
    for g in range(GROUPS):
        gb[:, g * 128:(g + 1) * 128] = gf[
            g * PITCH:g * PITCH + TOKENS, :
        ].astype(jnp.bfloat16)
    inner_acc[...] = jnp.zeros_like(inner_acc)
    weight_step(6)
    weight_end()

    def project(d, part):
        target = (x + d) % NX

        def columns(n, _):
            pair = [
                wg[target, 2 * n + i].reshape(WIDTH, 128) for i in range(2)
            ]
            term = jnp.dot(
                gb[...], jnp.concatenate(pair, axis=1),
                preferred_element_type=jnp.float32,
            ).astype(jnp.bfloat16)
            part[:, pl.ds(pl.multiple_of(n * 256, 256), 256)] = term
            wide = term.astype(jnp.float32)
            at = target * NY + 2 * n
            inner_acc[...] += (
                wide[:, :128] * dir_ref[pl.ds(at, 1), :]
                + wide[:, 128:] * dir_ref[pl.ds(at + 1, 1), :]
            )
            return 0

        lax.fori_loop(0, 4, columns, 0)

    top, low = pl.ds(0, 128), pl.ds(128, 128)
    right, left = at_x(1), at_x(NX - 1)
    project(2, part_o)
    x_copies = [
        remote(part_o.at[top], mid_l, x_send.at[0], x_recv.at[0], right),
        remote(part_o.at[low], mid_r, x_send.at[1], x_recv.at[1], left),
        remote(part_r.at[low], from_l.at[low], x_send.at[2], x_recv.at[2], right),
        remote(part_l.at[top], from_r.at[top], x_send.at[3], x_recv.at[3], left),
        remote(part_r.at[top], from_l.at[top], x_send.at[4], x_recv.at[4], right),
        remote(part_l.at[low], from_r.at[low], x_send.at[5], x_recv.at[5], left),
    ]
    x_copies[0].start()
    x_copies[1].start()
    project(1, part_r)
    x_copies[2].start()
    project(3, part_l)
    x_copies[3].start()
    project(0, part_own)
    inner_out[...] = lax.dot_general(
        jnp.ones((8, 128), jnp.float32), inner_acc[...],
        (((1,), (1,)), ((), ())), precision=HIGHEST,
        preferred_element_type=jnp.float32,
    )
    i_copies = [
        remote(inner_out, inner_in.at[d], i_send.at[d], i_recv.at[d], at_x(d))
        for d in range(1, NX)
    ]
    for copy in i_copies:
        copy.start()
    x_copies[0].wait_recv()
    part_r[0:128, :] = (
        part_r[0:128, :].astype(jnp.float32) + mid_l[...].astype(jnp.float32)
    ).astype(jnp.bfloat16)
    x_copies[4].start()
    x_copies[1].wait_recv()
    part_l[128:256, :] = (
        part_l[128:256, :].astype(jnp.float32) + mid_r[...].astype(jnp.float32)
    ).astype(jnp.bfloat16)
    x_copies[5].start()

    for copy in i_copies:
        copy.wait_recv()
    norm_total = jnp.sum(dir_ref[...] * dir_ref[...]) + EPSILON
    level = (inner_out[...] + inner_in[1] + inner_in[2] + inner_in[3]) / norm_total
    level_ref[...] = level
    level_wide = jnp.transpose(jnp.broadcast_to(level[0:1, :], (128, TOKENS)))
    weight_drain()
    halo.wait_send()
    for copy in y_copies + z_copies + i_copies:
        copy.wait_send()
    for index in range(2, 6):
        x_copies[index].wait_recv()
    for n in range(NY):
        cols = slice(n * 128, (n + 1) * 128)
        summed = (
            part_own[:, cols].astype(jnp.float32)
            + from_l[:, cols].astype(jnp.float32)
            + from_r[:, cols].astype(jnp.float32)
        )
        out_ref[:, cols] = (
            summed - level_wide * dir_ref[pl.ds(x * NY + n, 1), :]
        ).astype(jnp.bfloat16)
    for copy in x_copies:
        copy.wait_send()


def shards(q_feat, k_feat, v_feat, short_taps, decay_rate, residue, out_weight, direction):
    gains = residue * jnp.sqrt(-jnp.expm1(-2.0 * decay_rate)) * MODES ** (-0.5)
    rate_rows = decay_rate.T.reshape(MODES * GROUPS, 128)
    gain_rows = gains.T.reshape(MODES * GROUPS, 128)
    taps_rows = short_taps.reshape(9 * GROUPS, 128)
    f32, bf16 = jnp.float32, jnp.bfloat16
    vmem = pltpu.VMEM
    dma = pltpu.SemaphoreType.DMA
    ablated, level = pl.pallas_call(
        kernel,
        out_shape=(
            jax.ShapeDtypeStruct((TOKENS, WIDTH), bf16),
            jax.ShapeDtypeStruct((8, TOKENS), f32),
        ),
        in_specs=[pl.BlockSpec(memory_space=pltpu.VMEM)] * 8,
        out_specs=(pl.BlockSpec(memory_space=pltpu.VMEM),) * 2,
        scratch_shapes=[
            vmem((GROUPS * PITCH, 128), f32),
            vmem((GROUPS * PITCH, 128), f32),
            vmem((GROUPS * PITCH, 128), f32),
            vmem((TOKENS, GROUPS, 128), f32),
            vmem((TOKENS, GROUPS, 128), f32),
            vmem((GROUPS * PITCH, 128), f32),
            vmem((TOKENS, WIDTH), bf16),
            vmem((128, 128), f32),
            vmem((128, 128), f32),
            vmem((128, 128), f32),
            vmem((8, WIDTH), f32),
            vmem((8, WIDTH), f32),
            vmem((128, 128), bf16),
            vmem((NY, 128, 128), bf16),
            vmem((128, 128), bf16),
            vmem((NZ, 128, 128), bf16),
            vmem((NZ, NY, 2, 512, 128), bf16),
            vmem((TOKENS, WIDTH), bf16),
            vmem((TOKENS, WIDTH), bf16),
            vmem((TOKENS, WIDTH), bf16),
            vmem((TOKENS, WIDTH), bf16),
            vmem((128, WIDTH), bf16),
            vmem((128, WIDTH), bf16),
            vmem((TOKENS, WIDTH), bf16),
            vmem((TOKENS, WIDTH), bf16),
            vmem((TOKENS, 128), f32),
            vmem((8, TOKENS), f32),
            vmem((NX, 8, TOKENS), f32),
            dma((2,)), dma((NY,)), dma((NY,)), dma((NZ,)), dma((NZ,)),
            dma((12,)), dma((12,)), dma((9,)), dma((9,)),
            dma((6,)), dma((6,)), dma((NX,)), dma((NX,)),
        ],
        compiler_params=pltpu.CompilerParams(
            collective_id=0, has_side_effects=True, vmem_limit_bytes=48 << 20
        ),
        name="mixing",
    )(
        q_feat, k_feat, v_feat, taps_rows, rate_rows, gain_rows, out_weight,
        direction.reshape(32, 128),
    )
    return ablated, level[0]


def solution(mesh):
    placed = (
        P(("dp", "ctx"), "tp"),
        P(("dp", "ctx"), "tp"),
        P(("dp", "ctx"), "tp"),
        P(None, None, "tp"),
        P("tp", None),
        P("tp", None),
        P("tp", "ctx"),
        P(),
    )
    return jax.shard_map(
        shards,
        mesh=mesh,
        in_specs=placed,
        out_specs=(P(("dp", "ctx"), "tp"), P(("dp", "ctx"))),
        check_vma=False,
    )
```

time: 344 us -> 89 us (0.26)
  local copies, waits for them, and re-layouts: 161 us -> 6.15 us
  Pallas kernels: 0 us -> 80.9 us
  waiting for transfers between devices: 76.5 us -> 0 us
  blocking collectives: 28.6 us -> 0 us
  other arithmetic: 25.4 us -> 0.93 us
  matrix products: 19.7 us -> 0 us
  between operations: 15.3 us -> 0.69 us
  starting transfers between devices: 13.5 us -> 0 us
    pad x16 -> x0, local copies, waits for them, and re-layouts: 81.5 us -> none  [modal_filter(): lax.associative_scan(combine_modes, (block_decay, block_ends), axis=0)]
    pallas_call x0 -> x1, Pallas kernels: none -> 80.9 us  [shards(): pl.pallas_call(kernel, out_shape=(jax.ShapeDtypeStruct((TOKENS, WIDTH), b...]
    slice x21 -> x1, local copies, waits for them, and re-layouts: 46.1 us -> 0.56 us  [shards(): return (ablated, level[0])]
    all_to_all x1 -> x0, waiting for transfers between devices: 40.5 us -> none  [shards(): lax.all_to_all(stacked, 'ctx', split_axis=1, concat_axis=2, tiled=True)]
    reduce_scatter x1 -> x0, waiting for transfers between devices: 35.3 us -> none  [shards(): lax.psum_scatter(partial_terms.astype(jnp.bfloat16), 'tp', scatter_dimens...]
    unnamed x36 -> x11, local copies, waits for them, and re-layouts: 26.9 us -> 3.83 us
    all_to_all x1 -> x0, blocking collectives: 22.1 us -> none  [shards(): lax.all_to_all(gated_columns, 'ctx', split_axis=1, concat_axis=0, tiled=T...]
    dot_general x4 -> x0, matrix products: 19.7 us -> none  [the longest x1 8.99 us: modal_filter(): jnp.dot(scaled, lower_mask, precision=HIGHEST)]
  transfers between devices with their start and end apart: 3 -> 0, of which waited for: 2 -> 0; matrix products, arithmetic and copies ran while one was open for 57% -> 0% of each run, Pallas kernels for 0% -> 0%
where the time goes in v1:
time: 89 us; the launch traced here: 88.6 us
  Pallas kernels  80.9 us (91%)
  local copies, waits for them, and re-layouts  6.15 us (7%)
  other arithmetic  0.93 us (1%)
    pallas_call x1, Pallas kernels, shards(): pl.pallas_call(kernel, out_shape=(jax.ShapeDtypeStruct((TOKENS, WIDTH), b...  80.9 us
    unnamed x11, local copies, waits for them, and re-layouts  3.83 us

profile of v1, /device:TPU:1, one launch (start us, length us, event | category | flops | bytes accessed | tf_op | source)
XLA Modules:
  0.0 88.6 jit_solution(7399098652916182472)
XLA Ops:
  0.6 0.0 copy-start
  0.6 0.9 reshape.16.taps_ref
  1.5 0.9 %multiply_bitcast_fusion = f32[16,1024]{1,0:T(8,128)S(1)} fusion(f32[1024,16]{0,1:T(8,128)} %param.13, f32[1024,16]{0,1:T(8,128)} %param.12), kind=kLoop, calls=%fused_computation | loop fusion | flops 65536 | bytes 196608 | tf_op jit(solution)/shard_map/transpose | solution.py:390
  2.5 0.0 copy-start.4
  2.5 0.9 reshape.17.rate_ref
  3.3 0.0 copy-done
  3.4 0.0 copy-done.4
  3.4 0.0 copy-start.1
  3.4 1.0 %copy-done.1 = bf16[256,1024]{1,0:T(8,128)(2,1)S(1)} copy-done((bf16[256,1024]{1,0:T(8,128)(2,1)S(1)}, bf16[256,1024]{1,0:T(8,128)(2,1)}, u32[]{:S(2)}) %copy-start.1) | copy-done | bytes 524312
  4.4 0.0 copy-start.2
  4.4 1.0 %copy-done.2 = bf16[256,1024]{1,0:T(8,128)(2,1)S(1)} copy-done((bf16[256,1024]{1,0:T(8,128)(2,1)S(1)}, bf16[256,1024]{1,0:T(8,128)(2,1)}, u32[]{:S(2)}) %copy-start.2) | copy-done | bytes 524312
  5.5 0.0 copy-start.3
  5.5 0.9 %copy-done.3 = bf16[1024,128]{1,0:T(8,128)(2,1)S(1)} copy-done((bf16[1024,128]{1,0:T(8,128)(2,1)S(1)}, bf16[1024,128]{1,0:T(8,128)(2,1)}, u32[]{:S(2)}) %copy-start.3) | copy-done | bytes 262168
  6.4 80.9 %mixing.1 = (bf16[256,1024]{1,0:T(8,128)(2,1)S(1)}, f32[8,256]{1,0:T(8,128)S(1)}) custom-call(bf16[256,1024]{1,0:T(8,128)(2,1)S(1)} %copy-done, bf16[256,1024]{1,0:T(8,128)(2,1)S(1)} %copy-done.1, bf16[256,1024]{1,0:T(8,128)(2,1)S(1)} %copy-done.2, f32[72,128]{1,0:T(8,128)S(1)} %reshape.16.taps_ref, f32[128,128]{1,0:T(8,128)S(1)} %reshape.17.rate_ref, ...), custom_call_target="tpu_custom_call" | custom-call | tf_op jit(solution)/shard_map/mixing/pallas_call | solution.py:395
  87.3 0.6 slice.3
  87.9 0.8 copy.11
  (1 shorter events, 0.0 us)
Async XLA Ops:
  0.6 2.7 %copy-start = (bf16[256,1024]{1,0:T(8,128)(2,1)S(1)}, bf16[256,1024]{1,0:T(8,128)(2,1)}, u32[]{:S(2)}) copy-start(bf16[256,1024]{1,0:T(8,128)(2,1)} %q_ref.1) | copy-start | bytes 1572868
  2.5 0.9 %copy-start.4 = (f32[4096]{0:T(1024)S(1)}, f32[4096]{0:T(1024)}, u32[]{:S(2)}) copy-start(f32[4096]{0:T(1024)} %param.15) | copy-start | bytes 49156
  3.4 1.0 %copy-start.1 = (bf16[256,1024]{1,0:T(8,128)(2,1)S(1)}, bf16[256,1024]{1,0:T(8,128)(2,1)}, u32[]{:S(2)}) copy-start(bf16[256,1024]{1,0:T(8,128)(2,1)} %k_ref.1) | copy-start | bytes 1572868
  4.4 1.0 %copy-start.2 = (bf16[256,1024]{1,0:T(8,128)(2,1)S(1)}, bf16[256,1024]{1,0:T(8,128)(2,1)}, u32[]{:S(2)}) copy-start(bf16[256,1024]{1,0:T(8,128)(2,1)} %v_ref.1) | copy-start | bytes 1572868
  5.5 0.9 %copy-start.3 = (bf16[1024,128]{1,0:T(8,128)(2,1)S(1)}, bf16[1024,128]{1,0:T(8,128)(2,1)}, u32[]{:S(2)}) copy-start(bf16[1024,128]{1,0:T(8,128)(2,1)} %w_ref.1) | copy-start | bytes 786436

commit v2 on v1

--- a/solution.py
+++ b/solution.py
@@ -18,13 +18,15 @@
 
 
 def kernel(
-    q_ref, k_ref, v_ref, taps_ref, rate_ref, gain_ref, w_ref, dir_ref,
+    q_hbm, k_hbm, v_hbm, taps_hbm, rate_hbm, residue_hbm, w_hbm, dir_hbm,
     out_ref, level_ref,
-    xq, xk, xv, qs, ys, gf, gb, state, decay, carry,
+    q_ref, k_ref, v_ref, taps_in, rate_in, residue_in, dir_ref,
+    taps_ref, rate_ref, gain_ref,
+    xq, xk, xv, qs, us, ys, gf, gb, state, decay, carry,
     halo_out, halo_in, st_out, st_in, tot_out, tot_in,
     wg, part_o, part_r, part_l, part_own, mid_r, mid_l, from_l, from_r,
     inner_acc, inner_out, inner_in,
-    halo_sem, y_send, y_recv, z_send, z_recv, w_send, w_recv,
+    in_sem, halo_sem, y_send, y_recv, z_send, z_recv, w_send, w_recv,
     s_send, s_recv, x_send, x_recv, i_send, i_recv,
 ):
     dp = lax.axis_index("dp")
@@ -71,12 +73,24 @@
         pl.semaphore_signal(
             barrier, inc=1, device_id=target, device_id_type=pl.DeviceIdType.MESH
         )
-    wg[z, y, core] = w_ref[pl.ds(pl.multiple_of(core * 512, 512), 512), :]
+    loads = [
+        pltpu.make_async_copy(src, dst, in_sem.at[i])
+        for i, (src, dst) in enumerate((
+            (q_hbm, q_ref), (k_hbm, k_ref), (v_hbm, v_ref),
+            (w_hbm.at[pl.ds(0, 512)], wg.at[z, y, 0]),
+            (w_hbm.at[pl.ds(512, 512)], wg.at[z, y, 1]),
+            (rate_hbm, rate_in), (residue_hbm, residue_in), (taps_hbm, taps_in),
+            (dir_hbm, dir_ref),
+        ))
+    ]
+    for load in loads:
+        load.start()
+    for load in loads:
+        load.wait()
     halo_out[0:2, :] = q_ref[TOKENS - 16:, :].astype(jnp.float32)[14:16, :]
     halo_out[2:4, :] = k_ref[TOKENS - 16:, :].astype(jnp.float32)[14:16, :]
     halo_out[4:6, :] = v_ref[TOKENS - 16:, :].astype(jnp.float32)[14:16, :]
     halo_out[6:8, :] = jnp.zeros((2, WIDTH), jnp.float32)
-    pl.semaphore_wait(barrier, len(partners))
 
     def zz(d):
         return (z + d + NZ) % NZ
@@ -85,99 +99,183 @@
         return (y + d + NY) % NY
 
     lo, hi = pl.ds(0, 256), pl.ds(256, 256)
-    sent = [
-        [
-            (z, y, 0), (z, y, 0),
-            (zz(-1), y, 0, lo), (zz(1), y, 0, hi),
-            (slice(None), y, 0), (slice(None), y, 0),
-            (slice(None), yy(-1), 0), (slice(None), yy(1), 0),
-            (slice(None), yy(-2), 0), (slice(None), yy(2), 0),
-            (pl.ds(0, 2), yy(-3), 0), (pl.ds(2, 2), yy(3), 0),
-        ],
-        [
-            (z, y, 1), (z, y, 1),
-            (z, yy(-1), 1), (z, yy(1), 1),
-            (z, yy(-2), 1), (z, yy(2), 1),
-            (z, yy(-3), 1, lo), (z, yy(3), 1, hi),
-            (z, slice(None), 1), (z, slice(None), 1),
-            (zz(-1), pl.ds(0, 4), 1), (zz(1), pl.ds(4, 4), 1),
-        ],
-    ]
-    got = [
-        [
-            (zz(-1), y, 0), (zz(1), y, 0),
-            (zz(2), y, 0, lo), (zz(2), y, 0, hi),
-            (slice(None), yy(-1), 0), (slice(None), yy(1), 0),
-            (slice(None), yy(-2), 0), (slice(None), yy(2), 0),
-            (slice(None), yy(-3), 0), (slice(None), yy(3), 0),
-            (pl.ds(0, 2), yy(4), 0), (pl.ds(2, 2), yy(4), 0),
-        ],
-        [
-            (z, yy(-1), 1), (z, yy(1), 1),
-            (z, yy(-2), 1), (z, yy(2), 1),
-            (z, yy(-3), 1), (z, yy(3), 1),
-            (z, yy(4), 1, lo), (z, yy(4), 1, hi),
-            (zz(-1), slice(None), 1), (zz(1), slice(None), 1),
-            (zz(2), pl.ds(0, 4), 1), (zz(2), pl.ds(4, 4), 1),
-        ],
-    ]
-    axis_of = [["z"] * 4 + ["y"] * 8, ["y"] * 8 + ["z"] * 4]
-    to_sibling = [
-        [(2, [(slice(None), y, 0)])]
-        + [(3, got[0][4:6]), (4, got[0][6:8]), (5, got[0][8:10]), (6, got[0][10:12])],
-        [(4, [(z, slice(None), 1)]), (5, got[1][8:10]), (6, got[1][10:12])],
-    ]
-
-    def ring(role, index, slot):
-        sign = 1 if index % 2 == 0 else -1
-        target = at_y(NY + sign) if axis_of[role][index] == "y" else on_z_ring(sign)
-        region = wg.at[slot]
-        return remote(region, region, w_send.at[index], w_recv.at[index], target)
-
-    def handed(role, wanted=None):
-        flat = []
-        for step, slots in to_sibling[role]:
-            for slot in slots:
-                flat.append((step, slot))
-        return [
-            remote(wg.at[slot], wg.at[slot], s_send.at[i], s_recv.at[i], sibling)
-            for i, (step, slot) in enumerate(flat)
-            if wanted is None or step == wanted
-        ]
-
-    def weight_step(step):
+    ring = [{}, {}]
+
+    def piece(role, name, sign, axis, sent, got):
+        ring[role][name] = (sign, axis, sent, got, len(ring[role]))
+
+    near = (0, -1, 1, 2)
+    last = {1: (0, -1), -1: (1, 2)}
+    for sign in (1, -1):
+        part = lo if sign > 0 else hi
+        piece(0, ("z", sign, 1), sign, "z", (z, y, 0), (zz(-sign), y, 0))
+        piece(0, ("z", sign, 2), sign, "z", (zz(-sign), y, 0, part), (zz(2), y, 0, part))
+        for s in range(1, 5):
+            for r in near if s < 4 else last[sign]:
+                piece(
+                    0, ("y", sign, s, r), sign, "y",
+                    (zz(r), yy(-sign * (s - 1)), 0), (zz(r), yy(-sign * s), 0),
+                )
+        for s in range(1, 4):
+            piece(
+                1, ("y", sign, s), sign, "y",
+                (z, yy(-sign * (s - 1)), 1), (z, yy(-sign * s), 1),
+            )
+        piece(
+            1, ("y", sign, 4), sign, "y",
+            (z, yy(-sign * 3), 1, part), (z, yy(4), 1, part),
+        )
+        for e in (0, -1, 1, -2, 2, -3, 3, 4):
+            piece(1, ("z", sign, 1, e), sign, "z", (z, yy(e), 1), (zz(-sign), yy(e), 1))
+            if (e >= 0 and e < 4) == (sign > 0):
+                piece(1, ("z", sign, 2, e), sign, "z", (zz(-sign), yy(e), 1), (zz(2), yy(e), 1))
+
+    handed = [[], []]
+
+    def events_of_upper():
+        def give(s, r, sign):
+            return ("give", (zz(r), yy(-sign * s), 0))
+
+        yield [("start", ("z", 1, 1)), ("start", ("z", -1, 1)),
+               ("start", ("y", 1, 1, 0)), ("start", ("y", -1, 1, 0))]
+        for sign in (1, -1):
+            r = -sign
+            yield [("wait", ("z", sign, 1)), ("start", ("z", sign, 2)),
+                   ("start", ("y", 1, 1, r)), ("start", ("y", -1, 1, r)), give(0, r, 1)]
+        for s in range(1, 5):
+            if s == 2:
+                pass
+            for r in near:
+                acts = []
+                for sign in (1, -1):
+                    if s == 4 and r not in last[sign]:
+                        continue
+                    acts.append(("wait", ("y", sign, s, r)))
+                    if ("y", sign, s + 1, r) in ring[0]:
+                        acts.append(("start", ("y", sign, s + 1, r)))
+                    acts.append(give(s, r, sign))
+                yield acts
+                if s == 1 and r == 0:
+                    yield [("wait", ("z", 1, 2)), ("wait", ("z", -1, 2)),
+                           ("start", ("y", 1, 1, 2)), ("start", ("y", -1, 1, 2)),
+                           give(0, 2, 1)]
+
+    def events_of_lower():
+        def both_z(e):
+            return [("start", ("z", 1, 1, e)), ("start", ("z", -1, 1, e))]
+
+        def z_near(e):
+            acts = []
+            for sign in (1, -1):
+                acts.append(("wait", ("z", sign, 1, e)))
+                if ("z", sign, 2, e) in ring[1]:
+                    acts.append(("start", ("z", sign, 2, e)))
+                acts.append(("give", (zz(-sign), yy(e), 1)))
+            return acts
+
+        def z_far(e):
+            sign = 1 if ("z", 1, 2, e) in ring[1] else -1
+            return [("wait", ("z", sign, 2, e)), ("give", (zz(2), yy(e), 1))]
+
+        def y_near(s):
+            acts = []
+            for sign in (1, -1):
+                e = -sign * s
+                acts += [("wait", ("y", sign, s)), ("start", ("y", sign, s + 1))]
+                acts += both_z(e) + [("give", (z, yy(e), 1))]
+            return acts
+
+        yield [("start", ("y", 1, 1)), ("start", ("y", -1, 1))] + both_z(0)
+        yield y_near(1)
+        yield z_near(0)
+        yield y_near(2)
+        yield z_near(-1)
+        yield z_near(1) + z_far(0)
+        yield y_near(3)
+        yield z_near(-2) + z_far(-1)
+        yield z_near(2) + z_far(1)
+        yield ([("wait", ("y", 1, 4)), ("wait", ("y", -1, 4))] + both_z(4)
+               + [("give", (z, yy(4), 1))])
+        yield z_near(-3) + z_far(-2)
+        yield z_near(3) + z_far(2)
+        yield z_near(4)
+        yield z_far(-3)
+        yield z_far(3)
+        yield z_far(4)
+
+    events = [list(events_of_upper()), list(events_of_lower())]
+    event_count = max(len(e) for e in events)
+    for role in range(2):
+        for acts in events[role]:
+            for kind, what in acts:
+                if kind == "give":
+                    handed[role].append(what)
+    done = [0]
+
+    def ring_copy(role, name):
+        sign, axis, sent, got, index = ring[role][name]
+        target = at_y(NY + sign) if axis == "y" else on_z_ring(sign)
+        return lambda slot: remote(
+            wg.at[slot], wg.at[slot], w_send.at[index], w_recv.at[index], target
+        )
+
+    def give_copy(role, index):
+        slot = wg.at[handed[role][index]]
+        return remote(slot, slot, s_send.at[index], s_recv.at[index], sibling)
+
+    given = [0, 0]
+
+    def pump(count):
+        first = done[0]
+        done[0] = min(first + count, event_count)
         for role in range(2):
             @pl.when(core == role)
             def _(role=role):
-                if step > 0:
-                    for index in (2 * step - 2, 2 * step - 1):
-                        ring(role, index, got[role][index]).wait_recv()
-                if step < 6:
-                    for index in (2 * step, 2 * step + 1):
-                        ring(role, index, sent[role][index]).start()
-                for copy in handed(role, step):
-                    copy.start()
+                for acts in events[role][first:done[0]]:
+                    for kind, what in acts:
+                        if kind == "give":
+                            give_copy(role, given[role]).start()
+                            given[role] += 1
+                        elif kind == "start":
+                            ring_copy(role, what)(ring[role][what][2]).start()
+                        else:
+                            ring_copy(role, what)(ring[role][what][3]).wait_recv()
 
     def weight_end():
+        pump(event_count)
         for role in range(2):
             @pl.when(core == role)
             def _(role=role):
-                for copy in handed(1 - role):
-                    copy.wait_recv()
+                for index in range(len(handed[1 - role])):
+                    give_copy(1 - role, index).wait_recv()
 
     def weight_drain():
         for role in range(2):
             @pl.when(core == role)
             def _(role=role):
-                for index in range(12):
-                    ring(role, index, sent[role][index]).wait_send()
-                for copy in handed(role):
-                    copy.wait_send()
+                for name in ring[role]:
+                    ring_copy(role, name)(ring[role][name][2]).wait_send()
+                for index in range(len(handed[role])):
+                    give_copy(role, index).wait_send()
 
     halo = remote(halo_out, halo_in, halo_sem.at[0], halo_sem.at[1], after)
+    pl.semaphore_wait(barrier, len(partners))
     halo.start()
-    weight_step(0)
-
+    pump(1)
+
+    for g in range(GROUPS):
+        cols = slice(g * 128, (g + 1) * 128)
+        rate_ref[pl.ds(g, MODES, stride=GROUPS), :] = rate_in[:, cols]
+        doubled = 2.0 * rate_in[:, cols]
+        series = jnp.full_like(doubled, 1.0)
+        for k in range(9, 1, -1):
+            series = 1.0 - doubled * series * (1.0 / k)
+        grown = jnp.where(doubled < 0.25, doubled * series, 1.0 - jnp.exp(-doubled))
+        gain_ref[pl.ds(g, MODES, stride=GROUPS), :] = (
+            residue_in[:, cols] * jnp.sqrt(grown) * MODES ** (-0.5)
+        )
+        for f in range(3):
+            taps_ref[pl.ds(f * 3 * GROUPS + g, 3, stride=GROUPS), :] = taps_in[f, :, cols]
     for ref, full in ((q_ref, xq), (k_ref, xk), (v_ref, xv)):
         for g in range(GROUPS):
             full[g * PITCH + 8:(g + 1) * PITCH, :] = (
@@ -185,12 +283,6 @@
             )
     state[...] = jnp.zeros_like(state)
     decay[...] = jnp.exp(-rate_ref[...])
-    halo.wait_recv()
-    for i, full in enumerate((xq, xk, xv)):
-        for g in range(GROUPS):
-            rows = halo_in[2 * i:2 * i + 2, g * 128:(g + 1) * 128]
-            full[g * PITCH + 6:g * PITCH + 8, :] = jnp.where(ctx > 0, rows, 0.0)
-    weight_step(1)
 
     def row(t):
         return pl.ds(t, GROUPS, stride=PITCH)
@@ -198,7 +290,7 @@
     def tile(ref, i):
         return ref[i * GROUPS:(i + 1) * GROUPS, :]
 
-    def filter_step(i, _):
+    def scan_block(i):
         start = i * 8
         short = []
         for f, full in enumerate((xq, xk, xv)):
@@ -208,27 +300,54 @@
                 taps[0] * values[j + 2] + taps[1] * values[j + 1] + taps[2] * values[j]
                 for j in range(8)
             ])
+        signal = [short[1][j] * short[2][j] for j in range(8)]
         for j in range(8):
             qs[start + j] = short[0][j]
-        signal = [short[1][j] * short[2][j] for j in range(8)]
+            us[start + j] = signal[j]
+        return signal
+
+    def state_step(i, _):
+        signal = scan_block(i)
+        for m in range(MODES):
+            h = tile(state, m)
+            a = tile(decay, m)
+            for j in range(8):
+                h = a * h + signal[j]
+            state[m * GROUPS:(m + 1) * GROUPS, :] = h
+        return 0
+
+    def filter_step(i, _):
+        start = i * 8
+        signal = [us[start + j] for j in range(8)]
         total = [None] * 8
         for m in range(MODES):
-            h = tile(state, m)
+            h = tile(carry, m)
             a = tile(decay, m)
             c = tile(gain_ref, m)
             for j in range(8):
                 h = a * h + signal[j]
                 term = c * h
                 total[j] = term if total[j] is None else total[j] + term
-            state[m * GROUPS:(m + 1) * GROUPS, :] = h
+            carry[m * GROUPS:(m + 1) * GROUPS, :] = h
         for j in range(8):
             ys[start + j] = total[j]
         return 0
 
-    half = TOKENS // 16
-    lax.fori_loop(0, half, filter_step, 0)
-    weight_step(2)
-    lax.fori_loop(half, 2 * half, filter_step, 0)
+    blocks = TOKENS // 8
+    lax.fori_loop(1, blocks, state_step, 0)
+    halo.wait_recv()
+    for i, full in enumerate((xq, xk, xv)):
+        for g in range(GROUPS):
+            rows = halo_in[2 * i:2 * i + 2, g * 128:(g + 1) * 128]
+            full[g * PITCH + 6:g * PITCH + 8, :] = jnp.where(ctx > 0, rows, 0.0)
+    signal = scan_block(0)
+    for m in range(MODES):
+        a = tile(decay, m)
+        h = signal[0]
+        for j in range(1, 8):
+            h = a * h + signal[j]
+        rest = jnp.exp(-float(TOKENS - 8) * tile(rate_ref, m))
+        state[m * GROUPS:(m + 1) * GROUPS, :] = tile(state, m) + rest * h
 
     st_out[...] = state[...].astype(jnp.bfloat16)
     y_copies = [
@@ -238,7 +357,11 @@
     for copy in y_copies:
         copy.start()
     st_in[y] = st_out[...]
-    weight_step(3)
+    carry[...] = jnp.zeros_like(carry)
+    for quarter in range(4):
+        pump(1)
+        lax.fori_loop(quarter * blocks // 4, (quarter + 1) * blocks // 4, filter_step, 0)
+    pump(1)
     block_decay = jnp.exp(-float(TOKENS) * rate_ref[...])
     for d in range(1, NY):
         remote(
@@ -259,7 +382,7 @@
         copy.start()
     tot_in[z] = tot_out[...]
     carry[...] = prefix
-    weight_step(4)
+    pump(2)
     group_decay = jnp.exp(-float(TOKENS * NY) * rate_ref[...])
     own_decay = jnp.exp(-(TOKENS * y).astype(jnp.float32) * rate_ref[...])
     for d in range(1, NZ):
@@ -286,14 +409,15 @@
             gf[row(start + j), :] = qs[start + j] * total[j]
         return 0
 
-    lax.fori_loop(0, 2 * half, carry_step, 0)
-    weight_step(5)
+    pump(1)
+    for quarter in range(4):
+        lax.fori_loop(quarter * blocks // 4, (quarter + 1) * blocks // 4, carry_step, 0)
+        pump(1)
     for g in range(GROUPS):
         gb[:, g * 128:(g + 1) * 128] = gf[
             g * PITCH:g * PITCH + TOKENS, :
         ].astype(jnp.bfloat16)
     inner_acc[...] = jnp.zeros_like(inner_acc)
-    weight_step(6)
     weight_end()
 
     def project(d, part):
@@ -362,7 +486,7 @@
         copy.wait_recv()
     norm_total = jnp.sum(dir_ref[...] * dir_ref[...]) + EPSILON
     level = (inner_out[...] + inner_in[1] + inner_in[2] + inner_in[3]) / norm_total
-    level_ref[...] = level
+    level_ref[...] = level[0:1, :]
     level_wide = jnp.transpose(jnp.broadcast_to(level[0:1, :], (128, TOKENS)))
     weight_drain()
     halo.wait_send()
@@ -385,10 +509,6 @@
 
 
 def shards(q_feat, k_feat, v_feat, short_taps, decay_rate, residue, out_weight, direction):
-    gains = residue * jnp.sqrt(-jnp.expm1(-2.0 * decay_rate)) * MODES ** (-0.5)
-    rate_rows = decay_rate.T.reshape(MODES * GROUPS, 128)
-    gain_rows = gains.T.reshape(MODES * GROUPS, 128)
-    taps_rows = short_taps.reshape(9 * GROUPS, 128)
     f32, bf16 = jnp.float32, jnp.bfloat16
     vmem = pltpu.VMEM
     dma = pltpu.SemaphoreType.DMA
@@ -396,14 +516,25 @@
         kernel,
         out_shape=(
             jax.ShapeDtypeStruct((TOKENS, WIDTH), bf16),
-            jax.ShapeDtypeStruct((8, TOKENS), f32),
+            jax.ShapeDtypeStruct((1, TOKENS), f32),
         ),
-        in_specs=[pl.BlockSpec(memory_space=pltpu.VMEM)] * 8,
+        in_specs=[pl.BlockSpec(memory_space=pltpu.HBM)] * 8,
         out_specs=(pl.BlockSpec(memory_space=pltpu.VMEM),) * 2,
         scratch_shapes=[
+            vmem((TOKENS, WIDTH), bf16),
+            vmem((TOKENS, WIDTH), bf16),
+            vmem((TOKENS, WIDTH), bf16),
+            vmem((3, 3, WIDTH), f32),
+            vmem((MODES, WIDTH), f32),
+            vmem((MODES, WIDTH), f32),
+            vmem((32, 128), f32),
+            vmem((9 * GROUPS, 128), f32),
+            vmem((128, 128), f32),
+            vmem((128, 128), f32),
             vmem((GROUPS * PITCH, 128), f32),
             vmem((GROUPS * PITCH, 128), f32),
             vmem((GROUPS * PITCH, 128), f32),
+            vmem((TOKENS, GROUPS, 128), f32),
             vmem((TOKENS, GROUPS, 128), f32),
             vmem((TOKENS, GROUPS, 128), f32),
             vmem((GROUPS * PITCH, 128), f32),
@@ -429,19 +560,19 @@
             vmem((TOKENS, 128), f32),
             vmem((8, TOKENS), f32),
             vmem((NX, 8, TOKENS), f32),
-            dma((2,)), dma((NY,)), dma((NY,)), dma((NZ,)), dma((NZ,)),
-            dma((12,)), dma((12,)), dma((9,)), dma((9,)),
+            dma((9,)), dma((2,)), dma((NY,)), dma((NY,)), dma((NZ,)), dma((NZ,)),
+            dma((32,)), dma((32,)), dma((31,)), dma((31,)),
             dma((6,)), dma((6,)), dma((NX,)), dma((NX,)),
         ],
         compiler_params=pltpu.CompilerParams(
-            collective_id=0, has_side_effects=True, vmem_limit_bytes=48 << 20
+            collective_id=0, has_side_effects=True, vmem_limit_bytes=63 << 20
         ),
         name="mixing",
     )(
-        q_feat, k_feat, v_feat, taps_rows, rate_rows, gain_rows, out_weight,
+        q_feat, k_feat, v_feat, short_taps, decay_rate.T, residue.T, out_weight,
         direction.reshape(32, 128),
     )
-    return ablated, level[0]
+    return ablated, level.reshape(TOKENS)
 
 
 def solution(mesh):

time: 89 us -> 74.8 us (0.84)
  Pallas kernels: 80.9 us -> 71.5 us
  local copies, waits for them, and re-layouts: 6.15 us -> 2.44 us
  other arithmetic: 0.93 us -> 0 us
    pallas_call x1, Pallas kernels: 80.9 us -> 71.5 us  [shards(): pl.pallas_call(kernel, out_shape=(jax.ShapeDtypeStruct((TOKENS, WIDTH), b...]
    reshape x3 -> x0, local copies, waits for them, and re-layouts: 1.76 us -> none  [the longest x1 0.88 us: shards(): taps_rows = short_taps.reshape(9 * GROUPS, 128)]
    unnamed x11 -> x4, local copies, waits for them, and re-layouts: 3.83 us -> 2.44 us
    transpose x1 -> x0, other arithmetic: 0.93 us -> none  [shards(): gain_rows = gains.T.reshape(MODES * GROUPS, 128)]
where the time goes in v2:
time: 74.8 us; the launch traced here: 74.6 us
  Pallas kernels  71.5 us (96%)
  local copies, waits for them, and re-layouts  2.44 us (3%)
    pallas_call x1, Pallas kernels, shards(): pl.pallas_call(kernel, out_shape=(jax.ShapeDtypeStruct((TOKENS, WIDTH), b...  71.5 us
    unnamed x4, local copies, waits for them, and re-layouts  2.44 us

profile of v2, /device:TPU:1, one launch (start us, length us, event | category | flops | bytes accessed | tf_op | source)
XLA Modules:
  0.0 74.6 jit_solution(14561901850692461931)
XLA Ops:
  0.6 71.5 %mixing.1 = (bf16[256,1024]{1,0:T(8,128)(2,1)}, f32[1,256]{1,0:T(1,128)}) custom-call(bf16[256,1024]{1,0:T(8,128)(2,1)} %q_hbm.1, bf16[256,1024]{1,0:T(8,128)(2,1)} %k_hbm.1, bf16[256,1024]{1,0:T(8,128)(2,1)} %v_hbm.1, f32[3,3,1024]{2,1,0:T(4,128)} %taps_hbm.1, f32[16,1024]{1,0:T(8,128)} %bitcast.4, f32[16,1024]{1,0:T(8,128)} %bitcast.5, ...), custom_call_target="tpu_custom_call" | custom-call | tf_op jit(solution)/shard_map/mixing/pallas_call | solution.py:515
  72.2 0.0 copy-start
  72.2 1.9 %copy.12 = bf16[256,1024]{1,0:T(8,128)(2,1)} copy(bf16[256,1024]{1,0:T(8,128)(2,1)} %get-tuple-element.8) | data formatting | bytes 1048576
  74.0 0.0 copy-done
  74.0 0.6 copy.13
Async XLA Ops:
  72.2 1.9 %copy-start = (f32[1,256]{1,0:T(1,128)S(1)}, f32[1,256]{1,0:T(1,128)}, u32[]{:S(2)}) copy-start(f32[1,256]{1,0:T(1,128)} %get-tuple-element.5) | copy-start | bytes 3076

commit v3 on v2

--- a/solution.py
+++ b/solution.py
@@ -15,6 +15,10 @@
 NY = 8
 NZ = 4
 NX = 4
+UPPER = 384
+LOWER = WIDTH - UPPER
+COLUMN_GROUPS = ((0, -1, 1), (-2, 2), (-3, 3), (4,))
+GROUP_START = (0, 384, 640, 896)
 
 
 def kernel(
@@ -77,8 +81,7 @@
         pltpu.make_async_copy(src, dst, in_sem.at[i])
         for i, (src, dst) in enumerate((
             (q_hbm, q_ref), (k_hbm, k_ref), (v_hbm, v_ref),
-            (w_hbm.at[pl.ds(0, 512)], wg.at[z, y, 0]),
-            (w_hbm.at[pl.ds(512, 512)], wg.at[z, y, 1]),
+            (w_hbm, wg.at[z, y]),
             (rate_hbm, rate_in), (residue_hbm, residue_in), (taps_hbm, taps_in),
             (dir_hbm, dir_ref),
         ))
@@ -98,7 +101,9 @@
     def yy(d):
         return (y + d + NY) % NY
 
-    lo, hi = pl.ds(0, 256), pl.ds(256, 256)
+    upper, lower = pl.ds(0, UPPER), pl.ds(UPPER, LOWER)
+    upper_part = {1: pl.ds(0, UPPER // 2), -1: pl.ds(UPPER // 2, UPPER // 2)}
+    lower_part = {1: pl.ds(UPPER, LOWER // 2), -1: pl.ds(UPPER + LOWER // 2, LOWER // 2)}
     ring = [{}, {}]
 
     def piece(role, name, sign, axis, sent, got):
@@ -107,44 +112,50 @@
     near = (0, -1, 1, 2)
     last = {1: (0, -1), -1: (1, 2)}
     for sign in (1, -1):
-        part = lo if sign > 0 else hi
-        piece(0, ("z", sign, 1), sign, "z", (z, y, 0), (zz(-sign), y, 0))
-        piece(0, ("z", sign, 2), sign, "z", (zz(-sign), y, 0, part), (zz(2), y, 0, part))
+        half = upper_part[sign]
+        piece(0, ("z", sign, 1), sign, "z", (z, y, upper), (zz(-sign), y, upper))
+        piece(0, ("z", sign, 2), sign, "z", (zz(-sign), y, half), (zz(2), y, half))
         for s in range(1, 5):
             for r in near if s < 4 else last[sign]:
                 piece(
                     0, ("y", sign, s, r), sign, "y",
-                    (zz(r), yy(-sign * (s - 1)), 0), (zz(r), yy(-sign * s), 0),
+                    (zz(r), yy(-sign * (s - 1)), upper), (zz(r), yy(-sign * s), upper),
                 )
         for s in range(1, 4):
             piece(
                 1, ("y", sign, s), sign, "y",
-                (z, yy(-sign * (s - 1)), 1), (z, yy(-sign * s), 1),
+                (z, yy(-sign * (s - 1)), lower), (z, yy(-sign * s), lower),
             )
-        piece(
-            1, ("y", sign, 4), sign, "y",
-            (z, yy(-sign * 3), 1, part), (z, yy(4), 1, part),
-        )
+        half = lower_part[sign]
+        piece(1, ("y", sign, 4), sign, "y", (z, yy(-sign * 3), half), (z, yy(4), half))
         for e in (0, -1, 1, -2, 2, -3, 3, 4):
-            piece(1, ("z", sign, 1, e), sign, "z", (z, yy(e), 1), (zz(-sign), yy(e), 1))
+            piece(
+                1, ("z", sign, 1, e), sign, "z", (z, yy(e), lower), (zz(-sign), yy(e), lower)
+            )
             if (e >= 0 and e < 4) == (sign > 0):
-                piece(1, ("z", sign, 2, e), sign, "z", (zz(-sign), yy(e), 1), (zz(2), yy(e), 1))
+                piece(
+                    1, ("z", sign, 2, e), sign, "z",
+                    (zz(-sign), yy(e), lower), (zz(2), yy(e), lower),
+                )
 
     handed = [[], []]
 
+    def group_of(e):
+        return max(abs(e) - 1, 0)
+
+    def give(r, e, rows):
+        return ("give", ((zz(r), yy(e), rows), group_of(e)))
+
     def events_of_upper():
-        def give(s, r, sign):
-            return ("give", (zz(r), yy(-sign * s), 0))
-
-        yield [("start", ("z", 1, 1)), ("start", ("z", -1, 1)),
-               ("start", ("y", 1, 1, 0)), ("start", ("y", -1, 1, 0))]
+        yield [("start", ("z", 1, 1)), ("start", ("z", -1, 1)), ]
         for sign in (1, -1):
             r = -sign
             yield [("wait", ("z", sign, 1)), ("start", ("z", sign, 2)),
-                   ("start", ("y", 1, 1, r)), ("start", ("y", -1, 1, r)), give(0, r, 1)]
+                   give(r, 0, upper)]
+        yield [("wait", ("z", 1, 2)), ("wait", ("z", -1, 2)), give(2, 0, upper)] + [
+            ("start", ("y", sign, 1, r)) for r in near for sign in (1, -1)
+        ]
         for s in range(1, 5):
-            if s == 2:
-                pass
             for r in near:
                 acts = []
                 for sign in (1, -1):
@@ -153,12 +164,8 @@
                     acts.append(("wait", ("y", sign, s, r)))
                     if ("y", sign, s + 1, r) in ring[0]:
                         acts.append(("start", ("y", sign, s + 1, r)))
-                    acts.append(give(s, r, sign))
+                    acts.append(give(r, -sign * s, upper))
                 yield acts
-                if s == 1 and r == 0:
-                    yield [("wait", ("z", 1, 2)), ("wait", ("z", -1, 2)),
-                           ("start", ("y", 1, 1, 2)), ("start", ("y", -1, 1, 2)),
-                           give(0, 2, 1)]
 
     def events_of_lower():
         def both_z(e):
@@ -170,19 +177,19 @@
                 acts.append(("wait", ("z", sign, 1, e)))
                 if ("z", sign, 2, e) in ring[1]:
                     acts.append(("start", ("z", sign, 2, e)))
-                acts.append(("give", (zz(-sign), yy(e), 1)))
+                acts.append(give(-sign, e, lower))
             return acts
 
         def z_far(e):
             sign = 1 if ("z", 1, 2, e) in ring[1] else -1
-            return [("wait", ("z", sign, 2, e)), ("give", (zz(2), yy(e), 1))]
+            return [("wait", ("z", sign, 2, e)), give(2, e, lower)]
 
         def y_near(s):
             acts = []
             for sign in (1, -1):
                 e = -sign * s
                 acts += [("wait", ("y", sign, s)), ("start", ("y", sign, s + 1))]
-                acts += both_z(e) + [("give", (z, yy(e), 1))]
+                acts += both_z(e) + [give(0, e, lower)]
             return acts
 
         yield [("start", ("y", 1, 1)), ("start", ("y", -1, 1))] + both_z(0)
@@ -195,22 +202,19 @@
         yield z_near(-2) + z_far(-1)
         yield z_near(2) + z_far(1)
         yield ([("wait", ("y", 1, 4)), ("wait", ("y", -1, 4))] + both_z(4)
-               + [("give", (z, yy(4), 1))])
+               + [give(0, 4, lower)])
         yield z_near(-3) + z_far(-2)
         yield z_near(3) + z_far(2)
-        yield z_near(4)
-        yield z_far(-3)
+        yield z_near(4) + z_far(-3)
         yield z_far(3)
         yield z_far(4)
 
     events = [list(events_of_upper()), list(events_of_lower())]
-    event_count = max(len(e) for e in events)
     for role in range(2):
         for acts in events[role]:
             for kind, what in acts:
                 if kind == "give":
                     handed[role].append(what)
-    done = [0]
 
     def ring_copy(role, name):
         sign, axis, sent, got, index = ring[role][name]
@@ -220,18 +224,20 @@
         )
 
     def give_copy(role, index):
-        slot = wg.at[handed[role][index]]
+        slot = wg.at[handed[role][index][0]]
         return remote(slot, slot, s_send.at[index], s_recv.at[index], sibling)
 
+    done = [0, 0]
     given = [0, 0]
 
-    def pump(count):
-        first = done[0]
-        done[0] = min(first + count, event_count)
+    def pump_to(*counts):
         for role in range(2):
+            first = done[role]
+            done[role] = max(first, min(counts[role], len(events[role])))
+
             @pl.when(core == role)
-            def _(role=role):
-                for acts in events[role][first:done[0]]:
+            def _(role=role, first=first):
+                for acts in events[role][first:done[role]]:
                     for kind, what in acts:
                         if kind == "give":
                             give_copy(role, given[role]).start()
@@ -241,13 +247,14 @@
                         else:
                             ring_copy(role, what)(ring[role][what][3]).wait_recv()
 
-    def weight_end():
-        pump(event_count)
+    def weight_group(group):
+        pump_to((8, 12, 16, 20)[group], (9, 12, 14, 15)[group])
         for role in range(2):
             @pl.when(core == role)
             def _(role=role):
-                for index in range(len(handed[1 - role])):
-                    give_copy(1 - role, index).wait_recv()
+                for index, (_slot, of) in enumerate(handed[1 - role]):
+                    if of == group:
+                        give_copy(1 - role, index).wait_recv()
 
     def weight_drain():
         for role in range(2):
@@ -261,7 +268,7 @@
     halo = remote(halo_out, halo_in, halo_sem.at[0], halo_sem.at[1], after)
     pl.semaphore_wait(barrier, len(partners))
     halo.start()
-    pump(1)
+    pump_to(1, 1)
 
     for g in range(GROUPS):
         cols = slice(g * 128, (g + 1) * 128)
@@ -335,6 +342,7 @@
 
     blocks = TOKENS // 8
     lax.fori_loop(1, blocks, state_step, 0)
+    pump_to(3, 3)
     halo.wait_recv()
     for i, full in enumerate((xq, xk, xv)):
         for g in range(GROUPS):
@@ -358,10 +366,11 @@
         copy.start()
     st_in[y] = st_out[...]
     carry[...] = jnp.zeros_like(carry)
-    for quarter in range(4):
-        pump(1)
-        lax.fori_loop(quarter * blocks // 4, (quarter + 1) * blocks // 4, filter_step, 0)
-    pump(1)
+    pump_to(4, 3)
+    for part in range(2):
+        lax.fori_loop(part * blocks // 2, (part + 1) * blocks // 2, filter_step, 0)
+        pump_to(4 + part, 4)
+    pump_to(6, 5)
     block_decay = jnp.exp(-float(TOKENS) * rate_ref[...])
     for d in range(1, NY):
         remote(
@@ -382,7 +391,7 @@
         copy.start()
     tot_in[z] = tot_out[...]
     carry[...] = prefix
-    pump(2)
+    pump_to(8, 6)
     group_decay = jnp.exp(-float(TOKENS * NY) * rate_ref[...])
     own_decay = jnp.exp(-(TOKENS * y).astype(jnp.float32) * rate_ref[...])
     for d in range(1, NZ):
@@ -409,57 +418,87 @@
             gf[row(start + j), :] = qs[start + j] * total[j]
         return 0
 
-    pump(1)
-    for quarter in range(4):
-        lax.fori_loop(quarter * blocks // 4, (quarter + 1) * blocks // 4, carry_step, 0)
-        pump(1)
+    lax.fori_loop(0, blocks, carry_step, 0)
     for g in range(GROUPS):
         gb[:, g * 128:(g + 1) * 128] = gf[
             g * PITCH:g * PITCH + TOKENS, :
         ].astype(jnp.bfloat16)
     inner_acc[...] = jnp.zeros_like(inner_acc)
-    weight_end()
-
-    def project(d, part):
-        target = (x + d) % NX
-
-        def columns(n, _):
-            pair = [
-                wg[target, 2 * n + i].reshape(WIDTH, 128) for i in range(2)
-            ]
-            term = jnp.dot(
-                gb[...], jnp.concatenate(pair, axis=1),
-                preferred_element_type=jnp.float32,
-            ).astype(jnp.bfloat16)
-            part[:, pl.ds(pl.multiple_of(n * 256, 256), 256)] = term
-            wide = term.astype(jnp.float32)
-            at = target * NY + 2 * n
-            inner_acc[...] += (
-                wide[:, :128] * dir_ref[pl.ds(at, 1), :]
-                + wide[:, 128:] * dir_ref[pl.ds(at + 1, 1), :]
-            )
-            return 0
-
-        lax.fori_loop(0, 4, columns, 0)
-
     top, low = pl.ds(0, 128), pl.ds(128, 128)
     right, left = at_x(1), at_x(NX - 1)
-    project(2, part_o)
-    x_copies = [
-        remote(part_o.at[top], mid_l, x_send.at[0], x_recv.at[0], right),
-        remote(part_o.at[low], mid_r, x_send.at[1], x_recv.at[1], left),
-        remote(part_r.at[low], from_l.at[low], x_send.at[2], x_recv.at[2], right),
-        remote(part_l.at[top], from_r.at[top], x_send.at[3], x_recv.at[3], left),
-        remote(part_r.at[top], from_l.at[top], x_send.at[4], x_recv.at[4], right),
-        remote(part_l.at[low], from_r.at[low], x_send.at[5], x_recv.at[5], left),
-    ]
-    x_copies[0].start()
-    x_copies[1].start()
-    project(1, part_r)
-    x_copies[2].start()
-    project(3, part_l)
-    x_copies[3].start()
-    project(0, part_own)
+
+    def span(group):
+        return pl.ds(GROUP_START[group], 128 * len(COLUMN_GROUPS[group]))
+
+    def project(d, part, group):
+        target = (x + d) % NX
+        at = [yy(e) for e in COLUMN_GROUPS[group]]
+        blocks_here = [wg[target, c] for c in at]
+        term = jnp.dot(
+            gb[...],
+            jnp.concatenate(blocks_here, axis=1) if len(at) > 1 else blocks_here[0],
+            preferred_element_type=jnp.float32,
+        ).astype(jnp.bfloat16)
+        part[:, span(group)] = term
+        wide = term.astype(jnp.float32)
+        found = inner_acc[...]
+        for i, c in enumerate(at):
+            found += (
+                wide[:, i * 128:(i + 1) * 128] * dir_ref[pl.ds(target * NY + c, 1), :]
+            )
+        inner_acc[...] = found
+
+    def x_copy(group, index):
+        cols = span(group)
+        src, dst, target = (
+            (part_o.at[top, cols], mid_l.at[:, cols], right),
+            (part_o.at[low, cols], mid_r.at[:, cols], left),
+            (part_r.at[low, cols], from_l.at[low, cols], right),
+            (part_l.at[top, cols], from_r.at[top, cols], left),
+            (part_r.at[top, cols], from_l.at[top, cols], right),
+            (part_l.at[low, cols], from_r.at[low, cols], left),
+        )[index]
+        at = group * 6 + index
+        return remote(src, dst, x_send.at[at], x_recv.at[at], target)
+
+    def relay(group):
+        cols = span(group)
+        x_copy(group, 0).wait_recv()
+        part_r[0:128, cols] = (
+            part_r[0:128, cols].astype(jnp.float32) + mid_l[:, cols].astype(jnp.float32)
+        ).astype(jnp.bfloat16)
+        x_copy(group, 4).start()
+        x_copy(group, 1).wait_recv()
+        part_l[128:256, cols] = (
+            part_l[128:256, cols].astype(jnp.float32) + mid_r[:, cols].astype(jnp.float32)
+        ).astype(jnp.bfloat16)
+        x_copy(group, 5).start()
+
+    groups = len(COLUMN_GROUPS)
+    pace = (
+        ((10, 9), (11, 9), (12, 10), (12, 11)),
+        ((13, 12), (13, 12), (14, 13), (15, 13)),
+        ((16, 14), (17, 14), (18, 14), (18, 14)),
+        ((20, 15),) * 4,
+    )
+    for group in range(groups):
+        weight_group(group)
+        project(2, part_o, group)
+        x_copy(group, 0).start()
+        x_copy(group, 1).start()
+        pump_to(*pace[group][0])
+        project(1, part_r, group)
+        x_copy(group, 2).start()
+        pump_to(*pace[group][1])
+        project(3, part_l, group)
+        x_copy(group, 3).start()
+        if group in (1, 2):
+            relay(group - 1)
+        pump_to(*pace[group][2])
+        project(0, part_own, group)
+        pump_to(*pace[group][3])
+        if group == 2:
+            relay(group)
     inner_out[...] = lax.dot_general(
         jnp.ones((8, 128), jnp.float32), inner_acc[...],
         (((1,), (1,)), ((), ())), precision=HIGHEST,
@@ -471,17 +510,7 @@
     ]
     for copy in i_copies:
         copy.start()
-    x_copies[0].wait_recv()
-    part_r[0:128, :] = (
-        part_r[0:128, :].astype(jnp.float32) + mid_l[...].astype(jnp.float32)
-    ).astype(jnp.bfloat16)
-    x_copies[4].start()
-    x_copies[1].wait_recv()
-    part_l[128:256, :] = (
-        part_l[128:256, :].astype(jnp.float32) + mid_r[...].astype(jnp.float32)
-    ).astype(jnp.bfloat16)
-    x_copies[5].start()
-
+    relay(groups - 1)
     for copy in i_copies:
         copy.wait_recv()
     norm_total = jnp.sum(dir_ref[...] * dir_ref[...]) + EPSILON
@@ -492,20 +521,24 @@
     halo.wait_send()
     for copy in y_copies + z_copies + i_copies:
         copy.wait_send()
-    for index in range(2, 6):
-        x_copies[index].wait_recv()
-    for n in range(NY):
-        cols = slice(n * 128, (n + 1) * 128)
-        summed = (
-            part_own[:, cols].astype(jnp.float32)
-            + from_l[:, cols].astype(jnp.float32)
-            + from_r[:, cols].astype(jnp.float32)
-        )
-        out_ref[:, cols] = (
-            summed - level_wide * dir_ref[pl.ds(x * NY + n, 1), :]
-        ).astype(jnp.bfloat16)
-    for copy in x_copies:
-        copy.wait_send()
+    for group in range(groups):
+        for index in range(2, 6):
+            x_copy(group, index).wait_recv()
+        for i, e in enumerate(COLUMN_GROUPS[group]):
+            start = GROUP_START[group] + i * 128
+            cols = slice(start, start + 128)
+            summed = (
+                part_own[:, cols].astype(jnp.float32)
+                + from_l[:, cols].astype(jnp.float32)
+                + from_r[:, cols].astype(jnp.float32)
+            )
+            at = yy(e)
+            out_ref[:, pl.ds(pl.multiple_of(at * 128, 128), 128)] = (
+                summed - level_wide * dir_ref[pl.ds(x * NY + at, 1), :]
+            ).astype(jnp.bfloat16)
+    for group in range(groups):
+        for index in range(6):
+            x_copy(group, index).wait_send()
 
 
 def shards(q_feat, k_feat, v_feat, short_taps, decay_rate, residue, out_weight, direction):
@@ -548,7 +581,7 @@
             vmem((NY, 128, 128), bf16),
             vmem((128, 128), bf16),
             vmem((NZ, 128, 128), bf16),
-            vmem((NZ, NY, 2, 512, 128), bf16),
+            vmem((NZ, NY, WIDTH, 128), bf16),
             vmem((TOKENS, WIDTH), bf16),
             vmem((TOKENS, WIDTH), bf16),
             vmem((TOKENS, WIDTH), bf16),
@@ -560,9 +593,9 @@
             vmem((TOKENS, 128), f32),
             vmem((8, TOKENS), f32),
             vmem((NX, 8, TOKENS), f32),
-            dma((9,)), dma((2,)), dma((NY,)), dma((NY,)), dma((NZ,)), dma((NZ,)),
+            dma((8,)), dma((2,)), dma((NY,)), dma((NY,)), dma((NZ,)), dma((NZ,)),
             dma((32,)), dma((32,)), dma((31,)), dma((31,)),
-            dma((6,)), dma((6,)), dma((NX,)), dma((NX,)),
+            dma((24,)), dma((24,)), dma((NX,)), dma((NX,)),
         ],
         compiler_params=pltpu.CompilerParams(
             collective_id=0, has_side_effects=True, vmem_limit_bytes=63 << 20

time: 74.8 us -> 66.8 us (0.89)
  Pallas kernels: 71.5 us -> 63.6 us
    pallas_call x1, Pallas kernels: 71.5 us -> 63.6 us  [shards(): pl.pallas_call(kernel, out_shape=(jax.ShapeDtypeStruct((TOKENS, WIDTH), b...]
where the time goes in v3:
time: 66.8 us; the launch traced here: 66.7 us
  Pallas kernels  63.6 us (95%)
  local copies, waits for them, and re-layouts  2.44 us (4%)
    pallas_call x1, Pallas kernels, shards(): pl.pallas_call(kernel, out_shape=(jax.ShapeDtypeStruct((TOKENS, WIDTH), b...  63.6 us
    unnamed x4, local copies, waits for them, and re-layouts  2.44 us

profile of v3, /device:TPU:1, one launch (start us, length us, event | category | flops | bytes accessed | tf_op | source)
XLA Modules:
  0.0 66.7 jit_solution(7892293470163467459)
XLA Ops:
  0.6 63.6 %mixing.1 = (bf16[256,1024]{1,0:T(8,128)(2,1)}, f32[1,256]{1,0:T(1,128)}) custom-call(bf16[256,1024]{1,0:T(8,128)(2,1)} %q_hbm.1, bf16[256,1024]{1,0:T(8,128)(2,1)} %k_hbm.1, bf16[256,1024]{1,0:T(8,128)(2,1)} %v_hbm.1, f32[3,3,1024]{2,1,0:T(4,128)} %taps_hbm.1, f32[16,1024]{1,0:T(8,128)} %bitcast.4, f32[16,1024]{1,0:T(8,128)} %bitcast.5, ...), custom_call_target="tpu_custom_call" | custom-call | tf_op jit(solution)/shard_map/mixing/pallas_call | solution.py:548
  64.2 0.0 copy-start
  64.2 1.9 %copy.12 = bf16[256,1024]{1,0:T(8,128)(2,1)} copy(bf16[256,1024]{1,0:T(8,128)(2,1)} %get-tuple-element.8) | data formatting | bytes 1048576
  66.1 0.0 copy-done
  66.1 0.6 copy.13
Async XLA Ops:
  64.2 1.9 %copy-start = (f32[1,256]{1,0:T(1,128)S(1)}, f32[1,256]{1,0:T(1,128)}, u32[]{:S(2)}) copy-start(f32[1,256]{1,0:T(1,128)} %get-tuple-element.5) | copy-start | bytes 3076

commit v4 on v3

--- a/solution.py
+++ b/solution.py
@@ -15,7 +15,7 @@
 NY = 8
 NZ = 4
 NX = 4
-UPPER = 384
+UPPER = 416
 LOWER = WIDTH - UPPER
 COLUMN_GROUPS = ((0, -1, 1), (-2, 2), (-3, 3), (4,))
 GROUP_START = (0, 384, 640, 896)
@@ -103,7 +103,7 @@
 
     upper, lower = pl.ds(0, UPPER), pl.ds(UPPER, LOWER)
     upper_part = {1: pl.ds(0, UPPER // 2), -1: pl.ds(UPPER // 2, UPPER // 2)}
-    lower_part = {1: pl.ds(UPPER, LOWER // 2), -1: pl.ds(UPPER + LOWER // 2, LOWER // 2)}
+    lower_sub = (pl.ds(UPPER, LOWER // 2), pl.ds(UPPER + LOWER // 2, LOWER // 2))
     ring = [{}, {}]
 
     def piece(role, name, sign, axis, sent, got):
@@ -122,21 +122,28 @@
                     (zz(r), yy(-sign * (s - 1)), upper), (zz(r), yy(-sign * s), upper),
                 )
         for s in range(1, 4):
-            piece(
-                1, ("y", sign, s), sign, "y",
-                (z, yy(-sign * (s - 1)), lower), (z, yy(-sign * s), lower),
-            )
-        half = lower_part[sign]
-        piece(1, ("y", sign, 4), sign, "y", (z, yy(-sign * 3), half), (z, yy(4), half))
+            for k in range(2):
+                piece(
+                    1, ("y", sign, s, k), sign, "y",
+                    (z, yy(-sign * (s - 1)), lower_sub[k]), (z, yy(-sign * s), lower_sub[k]),
+                )
+        k = 0 if sign > 0 else 1
+        piece(
+            1, ("y", sign, 4, k), sign, "y",
+            (z, yy(-sign * 3), lower_sub[k]), (z, yy(4), lower_sub[k]),
+        )
         for e in (0, -1, 1, -2, 2, -3, 3, 4):
-            piece(
-                1, ("z", sign, 1, e), sign, "z", (z, yy(e), lower), (zz(-sign), yy(e), lower)
-            )
-            if (e >= 0 and e < 4) == (sign > 0):
+            for k in range(2):
+                rows = lower_sub[k]
                 piece(
-                    1, ("z", sign, 2, e), sign, "z",
-                    (zz(-sign), yy(e), lower), (zz(2), yy(e), lower),
+                    1, ("z", sign, 1, e, k), sign, "z",
+                    (z, yy(e), rows), (zz(-sign), yy(e), rows),
                 )
+                if (e >= 0 and e < 4) == (sign > 0):
+                    piece(
+                        1, ("z", sign, 2, e, k), sign, "z",
+                        (zz(-sign), yy(e), rows), (zz(2), yy(e), rows),
+                    )
 
     handed = [[], []]
 
@@ -168,31 +175,36 @@
                 yield acts
 
     def events_of_lower():
-        def both_z(e):
-            return [("start", ("z", 1, 1, e)), ("start", ("z", -1, 1, e))]
+        def both_z(e, k):
+            return [("start", ("z", sign, 1, e, k)) for sign in (1, -1)]
 
         def z_near(e):
             acts = []
-            for sign in (1, -1):
-                acts.append(("wait", ("z", sign, 1, e)))
-                if ("z", sign, 2, e) in ring[1]:
-                    acts.append(("start", ("z", sign, 2, e)))
-                acts.append(give(-sign, e, lower))
-            return acts
+            for k in range(2):
+                for sign in (1, -1):
+                    acts.append(("wait", ("z", sign, 1, e, k)))
+                    if ("z", sign, 2, e, k) in ring[1]:
+                        acts.append(("start", ("z", sign, 2, e, k)))
+            return acts + [give(-1, e, lower), give(1, e, lower)]
 
         def z_far(e):
-            sign = 1 if ("z", 1, 2, e) in ring[1] else -1
-            return [("wait", ("z", sign, 2, e)), give(2, e, lower)]
+            sign = 1 if ("z", 1, 2, e, 0) in ring[1] else -1
+            return [("wait", ("z", sign, 2, e, k)) for k in range(2)] + [give(2, e, lower)]
 
         def y_near(s):
             acts = []
-            for sign in (1, -1):
-                e = -sign * s
-                acts += [("wait", ("y", sign, s)), ("start", ("y", sign, s + 1))]
-                acts += both_z(e) + [give(0, e, lower)]
-            return acts
-
-        yield [("start", ("y", 1, 1)), ("start", ("y", -1, 1))] + both_z(0)
+            for k in range(2):
+                for sign in (1, -1):
+                    acts.append(("wait", ("y", sign, s, k)))
+                    if ("y", sign, s + 1, k) in ring[1]:
+                        acts.append(("start", ("y", sign, s + 1, k)))
+                for sign in (1, -1):
+                    acts += both_z(-sign * s, k)
+            return acts + [give(0, -s, lower), give(0, s, lower)]
+
+        yield [
+            ("start", ("y", sign, 1, k)) for k in range(2) for sign in (1, -1)
+        ] + both_z(0, 0) + both_z(0, 1)
         yield y_near(1)
         yield z_near(0)
         yield y_near(2)
@@ -201,8 +213,8 @@
         yield y_near(3)
         yield z_near(-2) + z_far(-1)
         yield z_near(2) + z_far(1)
-        yield ([("wait", ("y", 1, 4)), ("wait", ("y", -1, 4))] + both_z(4)
-               + [give(0, 4, lower)])
+        yield ([("wait", ("y", 1, 4, 0))] + both_z(4, 0) + [("wait", ("y", -1, 4, 1))]
+               + both_z(4, 1) + [give(0, 4, lower)])
         yield z_near(-3) + z_far(-2)
         yield z_near(3) + z_far(2)
         yield z_near(4) + z_far(-3)
@@ -238,7 +250,7 @@
             @pl.when(core == role)
             def _(role=role, first=first):
                 for acts in events[role][first:done[role]]:
-                    for kind, what in acts:
+                    for kind, what in sorted(acts, key=lambda act: act[0] == "give"):
                         if kind == "give":
                             give_copy(role, given[role]).start()
                             given[role] += 1
@@ -367,10 +379,10 @@
     st_in[y] = st_out[...]
     carry[...] = jnp.zeros_like(carry)
     pump_to(4, 3)
-    for part in range(2):
-        lax.fori_loop(part * blocks // 2, (part + 1) * blocks // 2, filter_step, 0)
-        pump_to(4 + part, 4)
-    pump_to(6, 5)
+    for part, counts in enumerate(((4, 3), (4, 4), (5, 5), (6, 5))):
+        lax.fori_loop(part * blocks // 4, (part + 1) * blocks // 4, filter_step, 0)
+        pump_to(*counts)
+    pump_to(7, 6)
     block_decay = jnp.exp(-float(TOKENS) * rate_ref[...])
     for d in range(1, NY):
         remote(
@@ -391,7 +403,7 @@
         copy.start()
     tot_in[z] = tot_out[...]
     carry[...] = prefix
-    pump_to(8, 6)
+    pump_to(8, 7)
     group_decay = jnp.exp(-float(TOKENS * NY) * rate_ref[...])
     own_decay = jnp.exp(-(TOKENS * y).astype(jnp.float32) * rate_ref[...])
     for d in range(1, NZ):
@@ -418,7 +430,10 @@
             gf[row(start + j), :] = qs[start + j] * total[j]
         return 0
 
-    lax.fori_loop(0, blocks, carry_step, 0)
+    lax.fori_loop(0, blocks // 2, carry_step, 0)
+    pump_to(9, 8)
+    lax.fori_loop(blocks // 2, blocks, carry_step, 0)
+    pump_to(11, 9)
     for g in range(GROUPS):
         gb[:, g * 128:(g + 1) * 128] = gf[
             g * PITCH:g * PITCH + TOKENS, :
@@ -594,7 +609,7 @@
             vmem((8, TOKENS), f32),
             vmem((NX, 8, TOKENS), f32),
             dma((8,)), dma((2,)), dma((NY,)), dma((NY,)), dma((NZ,)), dma((NZ,)),
-            dma((32,)), dma((32,)), dma((31,)), dma((31,)),
+            dma((62,)), dma((62,)), dma((31,)), dma((31,)),
             dma((24,)), dma((24,)), dma((NX,)), dma((NX,)),
         ],
         compiler_params=pltpu.CompilerParams(

time: 66.8 us -> 63.9 us (0.957)
  Pallas kernels: 63.6 us -> 60.6 us
    pallas_call x1, Pallas kernels: 63.6 us -> 60.6 us  [shards(): pl.pallas_call(kernel, out_shape=(jax.ShapeDtypeStruct((TOKENS, WIDTH), b...]
where the time goes in v4:
time: 63.9 us; the launch traced here: 63.7 us
  Pallas kernels  60.6 us (95%)
  local copies, waits for them, and re-layouts  2.44 us (4%)
  between operations  0.65 us (1%)
    pallas_call x1, Pallas kernels, shards(): pl.pallas_call(kernel, out_shape=(jax.ShapeDtypeStruct((TOKENS, WIDTH), b...  60.6 us
    unnamed x4, local copies, waits for them, and re-layouts  2.44 us

profile of v4, /device:TPU:1, one launch (start us, length us, event | category | flops | bytes accessed | tf_op | source)
XLA Modules:
  0.0 63.7 jit_solution(17087873004928662683)
XLA Ops:
  0.6 60.6 %mixing.1 = (bf16[256,1024]{1,0:T(8,128)(2,1)}, f32[1,256]{1,0:T(1,128)}) custom-call(bf16[256,1024]{1,0:T(8,128)(2,1)} %q_hbm.1, bf16[256,1024]{1,0:T(8,128)(2,1)} %k_hbm.1, bf16[256,1024]{1,0:T(8,128)(2,1)} %v_hbm.1, f32[3,3,1024]{2,1,0:T(4,128)} %taps_hbm.1, f32[16,1024]{1,0:T(8,128)} %bitcast.4, f32[16,1024]{1,0:T(8,128)} %bitcast.5, ...), custom_call_target="tpu_custom_call" | custom-call | tf_op jit(solution)/shard_map/mixing/pallas_call | solution.py:563
  61.2 0.0 copy-start
  61.2 1.9 %copy.12 = bf16[256,1024]{1,0:T(8,128)(2,1)} copy(bf16[256,1024]{1,0:T(8,128)(2,1)} %get-tuple-element.8) | data formatting | bytes 1048576
  63.1 0.0 copy-done
  63.1 0.6 copy.13
Async XLA Ops:
  61.2 1.9 %copy-start = (f32[1,256]{1,0:T(1,128)S(1)}, f32[1,256]{1,0:T(1,128)}, u32[]{:S(2)}) copy-start(f32[1,256]{1,0:T(1,128)} %get-tuple-element.5) | copy-start | bytes 3076

commit v5 on v4

--- a/solution.py
+++ b/solution.py
@@ -65,6 +65,16 @@
             device_id=target, device_id_type=pl.DeviceIdType.MESH,
         )
 
+    loads = [
+        pltpu.make_async_copy(src, dst, in_sem.at[i])
+        for i, (src, dst) in enumerate((
+            (w_hbm, wg.at[z, y]), (q_hbm, q_ref), (k_hbm, k_ref), (v_hbm, v_ref),
+            (rate_hbm, rate_in), (residue_hbm, residue_in), (taps_hbm, taps_in),
+            (dir_hbm, dir_ref),
+        ))
+    ]
+    for load in loads:
+        load.start()
     barrier = pltpu.get_barrier_semaphore()
     partners = (
         [at_y(d) for d in range(1, NY)]
@@ -77,24 +87,6 @@
         pl.semaphore_signal(
             barrier, inc=1, device_id=target, device_id_type=pl.DeviceIdType.MESH
         )
-    loads = [
-        pltpu.make_async_copy(src, dst, in_sem.at[i])
-        for i, (src, dst) in enumerate((
-            (q_hbm, q_ref), (k_hbm, k_ref), (v_hbm, v_ref),
-            (w_hbm, wg.at[z, y]),
-            (rate_hbm, rate_in), (residue_hbm, residue_in), (taps_hbm, taps_in),
-            (dir_hbm, dir_ref),
-        ))
-    ]
-    for load in loads:
-        load.start()
-    for load in loads:
-        load.wait()
-    halo_out[0:2, :] = q_ref[TOKENS - 16:, :].astype(jnp.float32)[14:16, :]
-    halo_out[2:4, :] = k_ref[TOKENS - 16:, :].astype(jnp.float32)[14:16, :]
-    halo_out[4:6, :] = v_ref[TOKENS - 16:, :].astype(jnp.float32)[14:16, :]
-    halo_out[6:8, :] = jnp.zeros((2, WIDTH), jnp.float32)
-
     def zz(d):
         return (z + d + NZ) % NZ
 
@@ -278,9 +270,16 @@
                     give_copy(role, index).wait_send()
 
     halo = remote(halo_out, halo_in, halo_sem.at[0], halo_sem.at[1], after)
+    loads[0].wait()
     pl.semaphore_wait(barrier, len(partners))
+    pump_to(1, 1)
+    for load in loads[1:]:
+        load.wait()
+    halo_out[0:2, :] = q_ref[TOKENS - 16:, :].astype(jnp.float32)[14:16, :]
+    halo_out[2:4, :] = k_ref[TOKENS - 16:, :].astype(jnp.float32)[14:16, :]
+    halo_out[4:6, :] = v_ref[TOKENS - 16:, :].astype(jnp.float32)[14:16, :]
+    halo_out[6:8, :] = jnp.zeros((2, WIDTH), jnp.float32)
     halo.start()
-    pump_to(1, 1)
 
     for g in range(GROUPS):
         cols = slice(g * 128, (g + 1) * 128)
@@ -374,8 +373,8 @@
         remote(st_out, st_in.at[y], y_send.at[d], y_recv.at[d], at_y(d))
         for d in range(1, NY)
     ]
-    for copy in y_copies:
-        copy.start()
+    for d in (4, 3, 5, 2, 6, 1, 7):
+        y_copies[d - 1].start()
     st_in[y] = st_out[...]
     carry[...] = jnp.zeros_like(carry)
     pump_to(4, 3)

time: 63.9 us -> 63.9 us (level)
  no operation moved by 1% of the time
where the time goes in v5:
time: 63.9 us; the launch traced here: 63.6 us
  Pallas kernels  60.5 us (95%)
  local copies, waits for them, and re-layouts  2.44 us (4%)
  between operations  0.65 us (1%)
    pallas_call x1, Pallas kernels, shards(): pl.pallas_call(kernel, out_shape=(jax.ShapeDtypeStruct((TOKENS, WIDTH), b...  60.5 us
    unnamed x4, local copies, waits for them, and re-layouts  2.44 us

profile of v5, /device:TPU:1, one launch (start us, length us, event | category | flops | bytes accessed | tf_op | source)
XLA Modules:
  0.0 63.6 jit_solution(13175391025485758821)
XLA Ops:
  0.6 60.5 %mixing.1 = (bf16[256,1024]{1,0:T(8,128)(2,1)}, f32[1,256]{1,0:T(1,128)}) custom-call(bf16[256,1024]{1,0:T(8,128)(2,1)} %q_hbm.1, bf16[256,1024]{1,0:T(8,128)(2,1)} %k_hbm.1, bf16[256,1024]{1,0:T(8,128)(2,1)} %v_hbm.1, f32[3,3,1024]{2,1,0:T(4,128)} %taps_hbm.1, f32[16,1024]{1,0:T(8,128)} %bitcast.4, f32[16,1024]{1,0:T(8,128)} %bitcast.5, ...), custom_call_target="tpu_custom_call" | custom-call | tf_op jit(solution)/shard_map/mixing/pallas_call | solution.py:562
  61.2 0.0 copy-start
  61.2 1.9 %copy.12 = bf16[256,1024]{1,0:T(8,128)(2,1)} copy(bf16[256,1024]{1,0:T(8,128)(2,1)} %get-tuple-element.8) | data formatting | bytes 1048576
  63.1 0.0 copy-done
  63.1 0.6 copy.13
Async XLA Ops:
  61.2 1.9 %copy-start = (f32[1,256]{1,0:T(1,128)S(1)}, f32[1,256]{1,0:T(1,128)}, u32[]{:S(2)}) copy-start(f32[1,256]{1,0:T(1,128)} %get-tuple-element.5) | copy-start | bytes 3076
